TPU v7x, 32 devices: a whole 2x2x4 slice. The times are simulated.
32 devices in a mesh: grp: 1, storm: 16 (over z, y, x), tile: 2 (over core).
Axes of the slice: x: 2, y: 2, z: 4, core: 2. Of those that a mesh axis runs over, the one named last changes fastest.
Arguments:
- patches: float32 [64, 2, 256, 256], P(('grp', 'storm', 'tile')), may hold values from -4 to 4
- patch_coeffs: float32 [64, 2], P(('grp', 'storm', 'tile')), may hold values from 0.01 to 0.15
- row_offset: int32 [64], P(('grp', 'storm', 'tile')), may hold values from 0 to 768, as said below
- col_offset: int32 [64], P(('grp', 'storm', 'tile')), may hold values from 0 to 1792
- live_counts: int32 [32], P(('grp', 'storm', 'tile')), may hold values from 0 to 2, as said below
- class_map: int32 [1024, 2048], P(('grp', 'storm'), 'tile'), may hold values from 0 to 15
- roughness: float32 [16], replicated, may hold values from 0.2 to 0.9
Outputs:
- smoothed_map: float32 [1024, 2048], P(('grp', 'storm'), 'tile')
Inputs may be any that keep to these rules, and one draw needn't show every extreme that they name: `live_counts`: A device's live patches are its first slots. The counts of the two devices whose storm indices differ by half the storm axis, at the same tile index, add up to 2. `row_offset`: each device's first half of its 2 slots lie wholly in the upper half of the map's 1024 rows and its other slots wholly in the lower half; the squares of one device's slots of one half all cover a common map row. So no aligned block of 64 map rows is covered by more than half of one device's slots, and some block is covered by exactly half of them on every device.
All inputs are finite; a program needn't handle non-finite values.
Results may differ from a plain program's by a relative error of at most 0.001.
The roundings to bfloat16 on the way count: a program that leaves them out, or rounds other values in their place, can miss the bound.
Values may be sent and summed in bfloat16 or wider, within the bound.
No kernel may reach another device: no remote copies, remote signals or barrier semaphores. Data moves between devices by JAX's collectives and lax.ppermute only.
A program may use at most 64 MiB of HBM per device.

v0:
```python
import functools

import jax
import jax.numpy as jnp
from jax import lax
from jax.experimental import pallas as pl
from jax.experimental.pallas import tpu as pltpu
from jax.sharding import PartitionSpec as P

STEPS = 6
CLASSES = 16
PASSES = 4
HALO = 8
LANES = 128
SMALL = pltpu.CompilerParams(vmem_limit_bytes=16 * 1024 * 1024)
F32 = jnp.float32
BF16 = jnp.bfloat16


def spread(side):
    column = lax.broadcasted_iota(jnp.int32, (side, side), 0)
    place = lax.broadcasted_iota(jnp.int32, (side, side), 1)
    parts = side // LANES
    return jnp.where(column == parts * lax.rem(place, LANES) + lax.div(place, LANES), 1.0, 0.0).astype(BF16)


def gather_turned(side, turn):
    place = lax.broadcasted_iota(jnp.int32, (side, side), 0)
    column = lax.broadcasted_iota(jnp.int32, (side, side), 1)
    parts = side // LANES
    moved = parts * lax.rem(place, LANES) + lax.div(place, LANES) + turn
    moved = jnp.where(moved >= side, moved - side, moved)
    return jnp.where(column == moved, 1.0, 0.0).astype(BF16)


def select_columns(x, one_hot):
    total = None
    for term in range(3):
        piece = x.astype(BF16)
        product = jnp.dot(piece, one_hot, preferred_element_type=F32)
        total = product if total is None else total + product
        if term < 2:
            x = x - piece.astype(F32)
    return total


def advance_into(source, drag, turn, bufs, gust, lead, side):
    tiles = side // HALO + 1
    count = side // LANES
    lane = lax.broadcasted_iota(jnp.int32, (HALO, LANES), 1)
    row = lax.broadcasted_iota(jnp.int32, (HALO, LANES), 0)
    first, last = lane == 0, lane == LANES - 1
    parts = [slice(c * LANES, (c + 1) * LANES) for c in range(count)]

    def sides(v):
        before = [jnp.where(first, 0.0, pltpu.roll(v[-1], 1, 1))] + v[:-1]
        after = v[1:] + [jnp.where(last, 0.0, pltpu.roll(v[0], LANES - 1, 1))]
        return [x + y for x, y in zip(before, after)]

    def put(buf, field, k, c, v):
        if k + (HALO - 1) * tiles >= side:
            v = jnp.where(row == HALO - 1, 0.0, v)
        buf[field, k + 1, :, parts[c]] = v
        if k == tiles - 1:
            buf[field, 0, :, parts[c]] = jnp.where(row == 0, 0.0, pltpu.roll(v, 1, 0))
        if k == 0:
            buf[field, tiles + 1, :, parts[c]] = jnp.where(row == HALO - 1, 0.0, pltpu.roll(v, HALO - 1, 0))

    for field in range(2):
        for k in range(tiles):
            for c in range(count):
                put(bufs[0], field, k, c, source[field, c, pl.ds(k, HALO, stride=tiles), :])
    turn = 5.0 * turn
    for step in range(STEPS):
        src, dst = bufs[step % 2], bufs[(step + 1) % 2]
        scale = 0.2**step
        pull = drag * (5.0 * scale)
        for k in range(tiles):
            e = [src[0, k + 1, :, p] for p in parts]
            n = [src[1, k + 1, :, p] for p in parts]
            side_e, side_n = sides(e), sides(n)
            for c, p in enumerate(parts):
                power = e[c] * e[c] + n[c] * n[c] + 0.25 / scale**2
                keep = 1.0 - pull * (power * lax.rsqrt(power))
                around_e = (src[0, k, :, p] + src[0, k + 2, :, p]) + side_e[c]
                around_n = (src[1, k, :, p] + src[1, k + 2, :, p]) + side_n[c]
                e_new = around_e + e[c] * keep + turn * n[c]
                n_new = around_n + n[c] * keep - turn * e[c]
                if step + 1 < STEPS:
                    put(dst, 0, k, c, e_new)
                    put(dst, 1, k, c, n_new)
                else:
                    power = e_new * e_new + n_new * n_new + 0.25 / (0.2 * scale) ** 2
                    v = (0.2 * scale) * (power * lax.rsqrt(power))
                    if k + (HALO - 1) * tiles >= side:
                        v = jnp.where(row == HALO - 1, 0.0, v)
                    gust[c, pl.ds(lead + k, HALO, stride=tiles), :] = v


def slabs_kernel(blocks, rows_dev, row_off, col_off, counts, coeffs, patches, out, loaded, buf_a, buf_b, gusts, sems):
    side = patches.shape[3]
    parts = side // LANES
    window = rows_dev + 2 * HALO

    def fetch(slot):
        return [
            pltpu.make_async_copy(
                patches.at[slot, field, :, pl.ds(c * LANES, LANES)],
                loaded.at[slot, field, c, pl.ds(0, side), :],
                sems.at[slot, field, c],
            )
            for field in range(2)
            for c in range(parts)
        ]

    for slot in range(2):

        @pl.when(counts[0] > slot)
        def _():
            for copy in fetch(slot):
                copy.start()

        loaded[slot, :, :, side:, :] = jnp.zeros((2, parts, HALO, LANES), F32)
        gusts[slot, :, 0:window, :] = jnp.zeros((parts, window, LANES), F32)
        gusts[slot, :, window + side :, :] = jnp.zeros((parts, window + HALO, LANES), F32)

    for slot in range(2):
        live = counts[0] > slot

        @pl.when(live)
        def _():
            for copy in fetch(slot):
                copy.wait()
            gusts[slot, :, window : window + HALO, :] = jnp.zeros((parts, HALO, LANES), F32)
            one_hot = spread(side)
            for field in range(2):
                both = jnp.concatenate([loaded[slot, field, c, 0:side, :] for c in range(parts)], axis=1)
                both = select_columns(both, one_hot)
                for c in range(parts):
                    loaded[slot, field, c, 0:side, :] = both[:, c * LANES : (c + 1) * LANES]
            advance_into(
                loaded.at[slot],
                coeffs[slot, 0],
                coeffs[slot, 1],
                (buf_a, buf_b),
                gusts.at[slot],
                window + lax.rem(row_off[slot], HALO),
                side,
            )
            body = slice(window, window + side + HALO)
            both = jnp.concatenate([gusts[slot, c, body, :] for c in range(parts)], axis=1).astype(BF16)
            both = jnp.dot(both, gather_turned(side, lax.rem(col_off[slot], side)), preferred_element_type=F32)
            for c in range(parts):
                gusts[slot, c, body, :] = both[:, c * LANES : (c + 1) * LANES]

        @pl.when(jnp.logical_not(live))
        def _():
            gusts[slot, :, window : window + side, :] = jnp.zeros((parts, side, LANES), F32)

    row = lax.broadcasted_iota(jnp.int32, (HALO, side), 0)
    lane = lax.broadcasted_iota(jnp.int32, (HALO, side), 1)
    place = []
    for slot in range(2):
        major = lax.div(col_off[slot], side)
        minor = col_off[slot] - major * side
        place.append((jnp.full((HALO, side), major.astype(F32)), jnp.where(lane >= minor, 1.0, 0.0)))

    def rows(slot, block, skip, count):
        base = lax.div(row_off[slot], HALO) * HALO
        at = jnp.clip(block * rows_dev - HALO - base, -window, side + HALO) + window + skip
        at = pl.ds(pl.multiple_of(at, HALO), count)
        return jnp.concatenate([gusts[slot, c, at, :] for c in range(parts)], axis=1)

    half = blocks // 2
    for block in range(blocks):
        main = 0 if block < half else 1
        other = 1 - main
        head = rows(other if block == half else main, block, 0, HALO)
        body = rows(main, block, HALO, rows_dev)
        tail = rows(other if block == half - 1 else main, block, HALO + rows_dev, HALO)
        head = jnp.where(row == 0, place[main][0], head)
        head = jnp.where(row == 1, place[main][1], head)
        head = jnp.where(row == 2, place[other][0], head)
        head = jnp.where(row == 3, place[other][1], head)
        out[block] = jnp.concatenate([head, body, tail], axis=0).astype(out.dtype)


def make_slabs(patches, coeffs, row_off, col_off, counts, blocks, rows_dev):
    side = patches.shape[3]
    parts = side // LANES
    window = rows_dev + 2 * HALO
    smem = pl.BlockSpec(memory_space=pltpu.SMEM)
    vmem = pl.BlockSpec(memory_space=pltpu.VMEM)
    return pl.pallas_call(
        functools.partial(slabs_kernel, blocks, rows_dev),
        name="slabs",
        compiler_params=SMALL,
        out_shape=jax.ShapeDtypeStruct((blocks, window, side), BF16),
        in_specs=[smem, smem, smem, smem, pl.BlockSpec(memory_space=pl.ANY)],
        out_specs=vmem,
        scratch_shapes=[
            pltpu.VMEM((2, 2, parts, side + HALO, LANES), F32),
            pltpu.VMEM((2, side // HALO + 3, HALO, side), F32),
            pltpu.VMEM((2, side // HALO + 3, HALO, side), F32),
            pltpu.VMEM((2, parts, side + 2 * window + HALO, LANES), F32),
            pltpu.SemaphoreType.DMA((2, 2, parts)),
        ],
        cost_estimate=pl.CostEstimate(flops=40 * STEPS * patches.size // 2, bytes_accessed=2 * patches.size, transcendentals=0),
    )(row_off, col_off, counts, coeffs, patches)


def stamp_kernel(cols_dev, map_cols, where, items, keep, give, strip):
    window, side = items.shape[1], items.shape[2]
    strip[...] = jnp.zeros_like(strip)
    upper_edge = where[1] == 1
    lower_edge = where[2] == 1
    tail_row = window - HALO
    cut = cols_dev + 2 * LANES

    def put(at, rows, value, mask):
        zero = jnp.zeros_like(value)
        col = pl.multiple_of(LANES + at * side, LANES)
        lo = (slice(rows, rows + value.shape[0]), pl.ds(col, side))
        hi = (slice(rows, rows + value.shape[0]), pl.ds(pl.multiple_of(col + side, LANES), side))
        strip[lo] = jnp.maximum(strip[lo], jnp.where(mask, value, zero))
        strip[hi] = jnp.maximum(strip[hi], jnp.where(mask, zero, value))

    count = items.shape[0]

    def column(item, at):
        return items[item, 0:16, 0:LANES].astype(F32)[at, 0].astype(jnp.int32)

    columns = [column(item, 0) for item in range(count)]
    for item in range(count):
        slab = items[item].astype(F32)
        head, body, tail = slab[0:HALO], slab[HALO:tail_row], slab[tail_row:]
        head = jnp.where(lower_edge, 0.0, head)
        tail = jnp.where(upper_edge, 0.0, tail)
        mask = slab[1:2, :] > 0.5
        put(columns[item], 0, jnp.concatenate([head, body, tail], axis=0), mask)

    def other(rows):
        columns = [column(item, 2) for item in range(count)]
        for item in range(count):
            mask = items[item, 0:HALO, :].astype(F32)[3:4, :] > 0.5
            put(columns[item], rows, items[item, rows : rows + HALO, :].astype(F32), mask)

    pl.when(lower_edge)(lambda: other(0))
    pl.when(upper_edge)(lambda: other(tail_row))

    own = pl.multiple_of(where[0] * cols_dev, LANES)
    away = pl.multiple_of((1 - where[0]) * cols_dev, LANES)
    keep[...] = strip[:, pl.ds(own, cut)].astype(keep.dtype)
    give[...] = strip[:, pl.ds(away, cut)].astype(give.dtype)


def stamp(items, where, cols_dev, map_cols):
    window, side = items.shape[1], items.shape[2]
    cut = cols_dev + 2 * LANES
    smem = pl.BlockSpec(memory_space=pltpu.SMEM)
    vmem = pl.BlockSpec(memory_space=pltpu.VMEM)
    return pl.pallas_call(
        functools.partial(stamp_kernel, cols_dev, map_cols),
        name="stamp",
        compiler_params=SMALL,
        out_shape=(jax.ShapeDtypeStruct((window, cut), BF16), jax.ShapeDtypeStruct((window, cut), BF16)),
        in_specs=[smem, vmem],
        out_specs=(vmem, vmem),
        scratch_shapes=[pltpu.VMEM((window, map_cols + 2 * LANES + side), F32)],
    )(where, items)


def blend_kernel(where, roughness, classes, above, below, beside, share):
    rows_dev, cols_dev = classes.shape
    tile = where[0]
    left = tile == 0

    def lookup(ids):
        weights = jnp.full(ids.shape, roughness[0])
        for level in range(1, CLASSES):
            weights = jnp.where(ids == float(level), roughness[level], weights)
        return 0.25 * weights

    inner = (HALO, HALO + rows_dev)
    has_above = where[3] == 1
    has_below = where[4] == 1
    mid = slice(LANES, LANES + cols_dev)
    edge = lookup(beside[...].astype(F32))
    row = lax.broadcasted_iota(jnp.int32, edge.shape, 0)
    bad = ((row < inner[0]) & jnp.logical_not(has_above)) | ((row >= inner[1]) & jnp.logical_not(has_below))
    edge = jnp.where(bad, 0.0, edge)
    share[:, 0:LANES] = jnp.where(left, 0.0, edge)
    share[:, LANES + cols_dev :] = jnp.where(left, edge, 0.0)
    share[0 : inner[0], mid] = jnp.where(has_above, lookup(above[...].astype(F32)), 0.0)
    share[inner[1] :, mid] = jnp.where(has_below, lookup(below[...].astype(F32)), 0.0)
    for at in range(0, rows_dev, 8):
        share[inner[0] + at : inner[0] + at + 8, mid] = lookup(classes[at : at + 8, :].astype(F32))


def smooth_kernel(where, keep, got, share, out, buf_a, buf_b):
    window, cut = keep.shape
    pad = HALO
    rows_dev, cols_dev = out.shape
    chunk = 8
    bufs = (buf_a, buf_b)
    for buf in bufs:
        buf[0:pad, :] = jnp.zeros((pad, cut), F32)
        buf[pad + window :, :] = jnp.zeros((pad, cut), F32)
    buf_a[pad : pad + window, :] = jnp.maximum(keep[...], got[...]).astype(F32)
    for step in range(PASSES):
        src, dst = bufs[step % 2], bufs[(step + 1) % 2]
        final = step + 1 == PASSES
        for row in range(HALO if final else 0, window - HALO if final else window, chunk):
            at = pad + row
            v = src[at : at + chunk, :]
            around = (
                src[at - 1 : at - 1 + chunk, :]
                + src[at + 1 : at + 1 + chunk, :]
                + pltpu.roll(v, 1, 1)
                + pltpu.roll(v, cut - 1, 1)
            )
            w = share[row : row + chunk, :]
            new = v - 4.0 * w * v + w * around
            if final:
                out[row - HALO : row - HALO + chunk, :] = new[:, LANES : LANES + cols_dev]
            else:
                dst[at : at + chunk, :] = jnp.where(w > 0.0, new, 0.0)


def on_device(patches, patch_coeffs, row_offset, col_offset, live_counts, class_map, roughness):
    storms = lax.axis_size("storm")
    rows_dev, cols_dev = class_map.shape
    tiles = lax.axis_size("tile")
    map_cols = cols_dev * tiles
    smem = pl.BlockSpec(memory_space=pltpu.SMEM)
    vmem = pl.BlockSpec(memory_space=pltpu.VMEM)
    side = patches.shape[3]
    window = rows_dev + 2 * HALO
    cut = cols_dev + 2 * LANES
    s = lax.axis_index("storm")
    t = lax.axis_index("tile")
    where = jnp.stack([t, s == storms // 2 - 1, s == storms // 2, s > 0, s < storms - 1]).astype(jnp.int32)

    slabs = make_slabs(patches, patch_coeffs, row_offset, col_offset, live_counts, storms, rows_dev)
    items = lax.all_to_all(slabs, "storm", split_axis=0, concat_axis=0, tiled=True)

    ids = class_map.astype(BF16)
    up = [(i + 1, i) for i in range(storms - 1)]
    down = [(i, i + 1) for i in range(storms - 1)]
    above = lax.ppermute(ids[rows_dev - HALO :], "storm", down)
    below = lax.ppermute(ids[:HALO], "storm", up)
    edge_col = jnp.where(t == 0, cols_dev - LANES, 0)
    tall = jnp.concatenate([above, ids, below], axis=0)
    beside = lax.ppermute(
        lax.dynamic_slice_in_dim(tall, edge_col, LANES, 1), "tile", [(0, 1), (1, 0)]
    )
    share = pl.pallas_call(
        blend_kernel,
        name="blend",
        compiler_params=SMALL,
        out_shape=jax.ShapeDtypeStruct((window, cut), F32),
        in_specs=[smem, smem, vmem, vmem, vmem, vmem],
        out_specs=vmem,
    )(where, roughness, class_map, above, below, beside)

    items, share = lax.optimization_barrier((items, share))
    keep, give = stamp(items, where, cols_dev, map_cols)
    got = lax.ppermute(give, "tile", [(0, 1), (1, 0)])
    return pl.pallas_call(
        smooth_kernel,
        name="smooth",
        compiler_params=SMALL,
        out_shape=jax.ShapeDtypeStruct((rows_dev, cols_dev), F32),
        in_specs=[smem, vmem, vmem, vmem],
        out_specs=vmem,
        scratch_shapes=[pltpu.VMEM((window + 2 * HALO, cut), F32)] * 2,
    )(where, keep, got, share)


def solution(mesh):
    return jax.shard_map(
        on_device,
        mesh=mesh,
        in_specs=(
            P(("grp", "storm", "tile"), None, None, None),
            P(("grp", "storm", "tile"), None),
            P(("grp", "storm", "tile")),
            P(("grp", "storm", "tile")),
            P(("grp", "storm", "tile")),
            P(("grp", "storm"), "tile"),
            P(),
        ),
        out_specs=P(("grp", "storm"), "tile"),
        check_vma=False,
    )
```

profile of v0, /device:TPU:17, one launch (start us, length us, event | category | flops | bytes accessed | tf_op | source)
XLA Modules:
  0.0 39.7 jit_solution(10787667804452967586)
XLA Ops:
  0.0 0.0 copy-start.3
  0.7 0.0 copy-done.3
  0.7 0.0 copy-done.2
  0.7 0.0 copy-start
  0.7 1.2 %copy-done = f32[2,2,256,256]{3,2,1,0:T(8,128)S(1)} copy-done((f32[2,2,256,256]{3,2,1,0:T(8,128)S(1)}, f32[2,2,256,256]{3,2,1,0:T(8,128)}, u32[]{:S(2)}) %copy-start) | copy-done | bytes 1048600
  1.9 0.7 %copy-done.4 = s32[2]{0:T(128)S(1)} copy-done((s32[2]{0:T(128)S(1)}, s32[2]{0:T(128)}, u32[]{:S(2)}) %copy-start.4) | copy-done | bytes 32
  2.6 3.8 %slabs.1 = bf16[16,80,256]{2,1,0:T(8,128)(2,1)} custom-call(s32[2]{0:T(128)S(1)} %copy-done.3, s32[2]{0:T(128)S(1)} %copy-done.4, s32[1]{0:T(128)S(6)} %copy.8.counts, f32[2,2]{1,0:T(2,128)S(1)} %copy-done.2, f32[2,2,256,256]{3,2,1,0:T(8,128)S(1)} %copy-done), custom_call_target="tpu_custom_call" | custom-call | flops 31457280 | bytes 524288 | tf_op jit(solution)/shard_map/slabs/pallas_call | solution.py:194
  6.4 0.0 copy-start.1
  6.4 8.0 %all-to-all-start = ((bf16[16,80,256]{2,1,0:T(8,128)(2,1)}), bf16[16,80,256]{2,1,0:T(8,128)(2,1)S(1)}, u32[]{:S(2)}, u32[]{:S(2)}) async-start(bf16[16,80,256]{2,1,0:T(8,128)(2,1)} %slabs.1), calls=%async_computation | async-start | bytes 1310720 | tf_op jit(solution)/shard_map/all_to_all | solution.py:345
  14.4 0.0 copy-done.1
  14.5 3.1 %collective-permute-start = (bf16[8,1024]{1,0:T(8,128)(2,1)S(1)}, bf16[8,1024]{1,0:T(8,128)(2,1)S(1)}, u32[]{:S(2)}, u32[]{:S(2)}) collective-permute-start(bf16[8,1024]{1,0:T(8,128)(2,1)S(1)} %get-tuple-element.14), channel_id=1, source_target_pairs={{0,2},{2,4},{4,6},{6,8},{8,10},{10,12},{12,14},{14,16},{16,18},{18... | collective-permute-start | bytes 49160 | tf_op jit(solution)/shard_map/ppermute | solution.py:350
  17.6 4.0 %collective-permute-start.1 = (bf16[8,1024]{1,0:T(8,128)(2,1)S(1)}, bf16[8,1024]{1,0:T(8,128)(2,1)S(1)}, u32[]{:S(2)}, u32[]{:S(2)}) collective-permute-start(bf16[8,1024]{1,0:T(8,128)(2,1)S(1)} %get-tuple-element.13), channel_id=1, source_target_pairs={{2,0},{4,2},{6,4},{8,6},{10,8},{12,10},{14,12},{16,14},{18,16},{20... | collective-permute-start | bytes 49160 | tf_op jit(solution)/shard_map/ppermute | solution.py:351
  21.6 9.9 %collective-permute-done.above = bf16[8,1024]{1,0:T(8,128)(2,1)S(1)} collective-permute-done((bf16[8,1024]{1,0:T(8,128)(2,1)S(1)}, bf16[8,1024]{1,0:T(8,128)(2,1)S(1)}, u32[]{:S(2)}, u32[]{:S(2)}) %collective-permute-start) | collective-permute-done | bytes 16416 | tf_op jit(solution)/shard_map/ppermute | solution.py:350
  31.5 0.0 collective-permute-done.1.below
  31.5 1.3 %collective-permute-start.2 = (bf16[80,128]{1,0:T(8,128)(2,1)S(1)}, bf16[80,128]{1,0:T(8,128)(2,1)S(1)}, u32[]{:S(2)}, u32[]{:S(2)}) collective-permute-start(bf16[80,128]{1,0:T(8,128)(2,1)S(1)} %fusion.1), channel_id=1, source_target_pairs={{0,1},{1,0},{2,3},{3,2},{4,5},{5,4},{6,7},{7,6},{8,9},{9,8},{10,11... | collective-permute-start | bytes 61448 | tf_op jit(solution)/shard_map/ppermute | solution.py:354
  32.8 0.1 stack.39.where
  32.9 0.8 %collective-permute-done.2.beside = bf16[80,128]{1,0:T(8,128)(2,1)S(1)} collective-permute-done((bf16[80,128]{1,0:T(8,128)(2,1)S(1)}, bf16[80,128]{1,0:T(8,128)(2,1)S(1)}, u32[]{:S(2)}, u32[]{:S(2)}) %collective-permute-start.2) | collective-permute-done | bytes 20512 | tf_op jit(solution)/shard_map/ppermute | solution.py:354
  33.7 0.0 copy-done.5
  33.7 0.9 %blend.1.share = f32[80,1280]{1,0:T(8,128)S(1)} custom-call(s32[5]{0:T(128)S(1)} %stack.39.where, f32[16]{0:T(128)S(1)} %copy-done.5, s32[64,1024]{1,0:T(8,128)S(1)} %copy-done.1, bf16[8,1024]{1,0:T(8,128)(2,1)S(1)} %collective-permute-done.above, bf16[8,1024]{1,0:T(8,128)(2,1)S(1)} %collective-permute-done.1.below, ...), custom_call_target="tpu_custom_call" | custom-call | tf_op jit(solution)/shard_map/blend/pallas_call | solution.py:357
  34.6 0.0 all-to-all-done.items
  34.6 1.2 %stamp.1 = (bf16[80,1280]{1,0:T(8,128)(2,1)S(1)}, bf16[80,1280]{1,0:T(8,128)(2,1)S(1)}) custom-call(s32[5]{0:T(128)S(1)} %stack.39.where, bf16[16,80,256]{2,1,0:T(8,128)(2,1)S(1)} %all-to-all-done.items), custom_call_target="tpu_custom_call" | custom-call | tf_op jit(solution)/shard_map/stamp/pallas_call | solution.py:262
  35.8 0.4 %collective-permute-start.3 = (bf16[80,1280]{1,0:T(8,128)(2,1)S(1)}, bf16[80,1280]{1,0:T(8,128)(2,1)S(1)}, u32[]{:S(2)}, u32[]{:S(2)}) collective-permute-start(bf16[80,1280]{1,0:T(8,128)(2,1)S(1)} %get-tuple-element.11), channel_id=1, source_target_pairs={{0,1},{1,0},{2,3},{3,2},{4,5},{5,4},{6,7},{7,6},{8,9},{9,8},{10,11... | collective-permute-start | bytes 614408 | tf_op jit(solution)/shard_map/ppermute | solution.py:368
  36.2 1.1 %collective-permute-done.3.got = bf16[80,1280]{1,0:T(8,128)(2,1)S(1)} collective-permute-done((bf16[80,1280]{1,0:T(8,128)(2,1)S(1)}, bf16[80,1280]{1,0:T(8,128)(2,1)S(1)}, u32[]{:S(2)}, u32[]{:S(2)}) %collective-permute-start.3) | collective-permute-done | bytes 204832 | tf_op jit(solution)/shard_map/ppermute | solution.py:368
  37.3 2.4 %smooth.1 = f32[64,1024]{1,0:T(8,128)} custom-call(s32[5]{0:T(128)S(1)} %stack.39.where, bf16[80,1280]{1,0:T(8,128)(2,1)S(1)} %get-tuple-element.10.keep, bf16[80,1280]{1,0:T(8,128)(2,1)S(1)} %collective-permute-done.3.got, f32[80,1280]{1,0:T(8,128)S(1)} %blend.1.share), custom_call_target="tpu_custom_call" | custom-call | tf_op jit(solution)/shard_map/smooth/pallas_call | solution.py:369
  (6 shorter events, 0.0 us)
Async XLA Ops:
  0.0 0.7 %copy-start.3 = (s32[2]{0:T(128)S(1)}, s32[2]{0:T(128)}, u32[]{:S(2)}) copy-start(s32[2]{0:T(128)} %row_off.1) | copy-start | bytes 28
  0.0 0.7 %copy-start.2 = (f32[2,2]{1,0:T(2,128)S(1)}, f32[2,2]{1,0:T(2,128)}, u32[]{:S(2)}) copy-start(f32[2,2]{1,0:T(2,128)} %coeffs.1) | copy-start | bytes 52
  0.7 1.2 %copy-start = (f32[2,2,256,256]{3,2,1,0:T(8,128)S(1)}, f32[2,2,256,256]{3,2,1,0:T(8,128)}, u32[]{:S(2)}) copy-start(f32[2,2,256,256]{3,2,1,0:T(8,128)} %patches.1) | copy-start | bytes 3145732
  1.9 0.7 %copy-start.4 = (s32[2]{0:T(128)S(1)}, s32[2]{0:T(128)}, u32[]{:S(2)}) copy-start(s32[2]{0:T(128)} %col_off.1) | copy-start | bytes 28
  6.4 8.0 %copy-start.1 = (s32[64,1024]{1,0:T(8,128)S(1)}, s32[64,1024]{1,0:T(8,128)}, u32[]{:S(2)}) copy-start(s32[64,1024]{1,0:T(8,128)} %classes.1) | copy-start | bytes 786436
  6.4 28.2 %all-to-all-start = ((bf16[16,80,256]{2,1,0:T(8,128)(2,1)}), bf16[16,80,256]{2,1,0:T(8,128)(2,1)S(1)}, u32[]{:S(2)}, u32[]{:S(2)}) async-start(bf16[16,80,256]{2,1,0:T(8,128)(2,1)} %slabs.1), calls=%async_computation | async-start | bytes 1310720 | tf_op jit(solution)/shard_map/all_to_all | solution.py:345
  14.5 17.0 %collective-permute-start = (bf16[8,1024]{1,0:T(8,128)(2,1)S(1)}, bf16[8,1024]{1,0:T(8,128)(2,1)S(1)}, u32[]{:S(2)}, u32[]{:S(2)}) collective-permute-start(bf16[8,1024]{1,0:T(8,128)(2,1)S(1)} %get-tuple-element.14), channel_id=1, source_target_pairs={{0,2},{2,4},{4,6},{6,8},{8,10},{10,12},{12,14},{14,16},{16,18},{18... | collective-permute-start | bytes 49160 | tf_op jit(solution)/shard_map/ppermute | solution.py:350
  17.6 13.9 %collective-permute-start.1 = (bf16[8,1024]{1,0:T(8,128)(2,1)S(1)}, bf16[8,1024]{1,0:T(8,128)(2,1)S(1)}, u32[]{:S(2)}, u32[]{:S(2)}) collective-permute-start(bf16[8,1024]{1,0:T(8,128)(2,1)S(1)} %get-tuple-element.13), channel_id=1, source_target_pairs={{2,0},{4,2},{6,4},{8,6},{10,8},{12,10},{14,12},{16,14},{18,16},{20... | collective-permute-start | bytes 49160 | tf_op jit(solution)/shard_map/ppermute | solution.py:351
  31.5 2.1 %collective-permute-start.2 = (bf16[80,128]{1,0:T(8,128)(2,1)S(1)}, bf16[80,128]{1,0:T(8,128)(2,1)S(1)}, u32[]{:S(2)}, u32[]{:S(2)}) collective-permute-start(bf16[80,128]{1,0:T(8,128)(2,1)S(1)} %fusion.1), channel_id=1, source_target_pairs={{0,1},{1,0},{2,3},{3,2},{4,5},{5,4},{6,7},{7,6},{8,9},{9,8},{10,11... | collective-permute-start | bytes 61448 | tf_op jit(solution)/shard_map/ppermute | solution.py:354
  32.8 0.8 %copy-start.5 = (f32[16]{0:T(128)S(1)}, f32[16]{0:T(128)}, u32[]{:S(2)}) copy-start(f32[16]{0:T(128)} %roughness.1) | copy-start | bytes 196
  35.8 1.5 %collective-permute-start.3 = (bf16[80,1280]{1,0:T(8,128)(2,1)S(1)}, bf16[80,1280]{1,0:T(8,128)(2,1)S(1)}, u32[]{:S(2)}, u32[]{:S(2)}) collective-permute-start(bf16[80,1280]{1,0:T(8,128)(2,1)S(1)} %get-tuple-element.11), channel_id=1, source_target_pairs={{0,1},{1,0},{2,3},{3,2},{4,5},{5,4},{6,7},{7,6},{8,9},{9,8},{10,11... | collective-permute-start | bytes 614408 | tf_op jit(solution)/shard_map/ppermute | solution.py:368
where the time goes:
time: 39.6 us; the launch traced here: 39.7 us
  starting transfers between devices  16.7 us (42%)
  waiting for transfers between devices  11.8 us (30%)
  Pallas kernels  8.38 us (21%)
  local copies, waits for them, and re-layouts  1.98 us (5%)
  between operations  0.79 us (2%)
    ppermute x1, waiting for transfers between devices, on_device(): above = lax.ppermute(ids[rows_dev - HALO:], 'storm', down)  9.94 us
    all_to_all x1, starting transfers between devices, on_device(): lax.all_to_all(slabs, 'storm', split_axis=0, concat_axis=0, tiled=True)  7.97 us
    ppermute x1, starting transfers between devices, on_device(): below = lax.ppermute(ids[:HALO], 'storm', up)  3.99 us
    pallas_call x1, Pallas kernels, make_slabs(): pl.pallas_call(functools.partial(slabs_kernel, blocks, rows_dev), name='s...  3.84 us
    ppermute x1, starting transfers between devices, on_device(): above = lax.ppermute(ids[rows_dev - HALO:], 'storm', down)  3.09 us
    pallas_call x1, Pallas kernels, on_device(): pl.pallas_call(smooth_kernel, name='smooth', compiler_params=SMALL, out_s...  2.45 us
    unnamed x12, local copies, waits for them, and re-layouts  1.89 us
    ppermute x1, starting transfers between devices, on_device(): lax.ppermute(lax.dynamic_slice_in_dim(tall, edge_col, LANES, 1), 'tile',...  1.29 us
  transfers between devices with their start and end apart: 5, of which 3 were waited for; matrix products, arithmetic and copies ran while one was open for 0% of the time, Pallas kernels for 2%

commit v1 on v0

v1 whole, which is shorter than its diff:
```python
import functools

import jax
import jax.numpy as jnp
from jax import lax
from jax.experimental import pallas as pl
from jax.experimental.pallas import tpu as pltpu
from jax.sharding import PartitionSpec as P


STEPS = 6
CLASSES = 16
PASSES = 4
HALO = 8
LANES = 128
SEND_ROWS = 16
SMALL = pltpu.CompilerParams(vmem_limit_bytes=16 * 1024 * 1024)
F32 = jnp.float32
BF16 = jnp.bfloat16


def spread(side):
    column = lax.broadcasted_iota(jnp.int32, (side, side), 0)
    place = lax.broadcasted_iota(jnp.int32, (side, side), 1)
    parts = side // LANES
    return jnp.where(column == parts * lax.rem(place, LANES) + lax.div(place, LANES), 1.0, 0.0).astype(BF16)


def gather_turned(side, turn):
    place = lax.broadcasted_iota(jnp.int32, (side, side), 0)
    column = lax.broadcasted_iota(jnp.int32, (side, side), 1)
    parts = side // LANES
    moved = parts * lax.rem(place, LANES) + lax.div(place, LANES) + turn
    moved = jnp.where(moved >= side, moved - side, moved)
    return jnp.where(column == moved, 1.0, 0.0).astype(BF16)


def select_columns(x, one_hot):
    total = None
    for term in range(3):
        piece = x.astype(BF16)
        product = jnp.dot(piece, one_hot, preferred_element_type=F32)
        total = product if total is None else total + product
        if term < 2:
            x = x - piece.astype(F32)
    return total


def advance_into(source, drag, turn, bufs, gust, lead, side):
    tiles = side // HALO + 1
    count = side // LANES
    lane = lax.broadcasted_iota(jnp.int32, (HALO, LANES), 1)
    row = lax.broadcasted_iota(jnp.int32, (HALO, LANES), 0)
    first, last = lane == 0, lane == LANES - 1
    parts = [slice(c * LANES, (c + 1) * LANES) for c in range(count)]

    def sides(v):
        before = [jnp.where(first, 0.0, pltpu.roll(v[-1], 1, 1))] + v[:-1]
        after = v[1:] + [jnp.where(last, 0.0, pltpu.roll(v[0], LANES - 1, 1))]
        return [x + y for x, y in zip(before, after)]

    def put(buf, field, k, c, v):
        if k + (HALO - 1) * tiles >= side:
            v = jnp.where(row == HALO - 1, 0.0, v)
        buf[field, k + 1, :, parts[c]] = v
        if k == tiles - 1:
            buf[field, 0, :, parts[c]] = jnp.where(row == 0, 0.0, pltpu.roll(v, 1, 0))
        if k == 0:
            buf[field, tiles + 1, :, parts[c]] = jnp.where(row == HALO - 1, 0.0, pltpu.roll(v, HALO - 1, 0))

    for field in range(2):
        for k in range(tiles):
            for c in range(count):
                put(bufs[0], field, k, c, source[field, c, pl.ds(k, HALO, stride=tiles), :])
    turn = 5.0 * turn
    for step in range(STEPS):
        src, dst = bufs[step % 2], bufs[(step + 1) % 2]
        scale = 0.2**step
        pull = drag * (5.0 * scale)
        for k in range(tiles):
            e = [src[0, k + 1, :, p] for p in parts]
            n = [src[1, k + 1, :, p] for p in parts]
            side_e, side_n = sides(e), sides(n)
            for c, p in enumerate(parts):
                power = e[c] * e[c] + n[c] * n[c] + 0.25 / scale**2
                keep = 1.0 - pull * (power * lax.rsqrt(power))
                around_e = (src[0, k, :, p] + src[0, k + 2, :, p]) + side_e[c]
                around_n = (src[1, k, :, p] + src[1, k + 2, :, p]) + side_n[c]
                e_new = around_e + e[c] * keep + turn * n[c]
                n_new = around_n + n[c] * keep - turn * e[c]
                if step + 1 < STEPS:
                    put(dst, 0, k, c, e_new)
                    put(dst, 1, k, c, n_new)
                else:
                    power = e_new * e_new + n_new * n_new + 0.25 / (0.2 * scale) ** 2
                    v = (0.2 * scale) * (power * lax.rsqrt(power))
                    if k + (HALO - 1) * tiles >= side:
                        v = jnp.where(row == HALO - 1, 0.0, v)
                    gust[c, pl.ds(lead + k, HALO, stride=tiles), :] = v


def slabs_kernel(
    hops,
    rows_dev,
    counts,
    row_hbm,
    col_hbm,
    coeffs_hbm,
    classes,
    patches,
    own,
    give,
    row_off,
    col_off,
    coeffs,
    loaded,
    buf_a,
    buf_b,
    gusts,
    edges,
    sems,
    small_sems,
):
    smalls = [
        pltpu.make_async_copy(source, target, small_sems.at[i])
        for i, (source, target) in enumerate(
            (
                (row_hbm, row_off),
                (col_hbm, col_off),
                (coeffs_hbm, coeffs),
                (classes.at[pl.ds(0, HALO), :], edges.at[0]),
                (classes.at[pl.ds(rows_dev - HALO, HALO), :], edges.at[1]),
            )
        )
    ]
    for copy in smalls:
        copy.start()
    side = patches.shape[3]
    parts = side // LANES
    window = rows_dev + 2 * HALO
    half = len(hops)
    storm, tile = lax.axis_index("storm"), lax.axis_index("tile")

    def fetch(slot, field):
        return [
            pltpu.make_async_copy(
                patches.at[slot, field, :, pl.ds(c * LANES, LANES)],
                loaded.at[slot, field, c, pl.ds(0, side), :],
                sems.at[slot, field, c],
            )
            for c in range(parts)
        ]

    for slot in range(2):

        @pl.when(counts[0] > slot)
        def _():
            for field in range(2):
                for copy in fetch(slot, field):
                    copy.start()

    row = lax.broadcasted_iota(jnp.int32, (HALO, side), 0)
    lane = lax.broadcasted_iota(jnp.int32, (HALO, side), 1)
    for slot in range(2):
        loaded[slot, :, :, side:, :] = jnp.zeros((2, parts, loaded.shape[3] - side, LANES), F32)
        gusts[slot, :, 0:window, :] = jnp.zeros((parts, window, LANES), F32)
        gusts[slot, :, window + side :, :] = jnp.zeros((parts, window + HALO, LANES), F32)

    def rows(slot, block, skip, count):
        base = lax.div(row_off[slot], HALO) * HALO
        at = jnp.clip(block * rows_dev - HALO - base, -window, side + HALO) + window + skip
        at = pl.ds(pl.multiple_of(at, HALO), count)
        return jnp.concatenate([gusts[slot, c, at, :] for c in range(parts)], axis=1)

    def build(out, item, block):
        main = jnp.where(block < half, 0, 1)
        other = 1 - main
        head = rows(jnp.where(block == half, other, main), block, 0, HALO)
        body = rows(main, block, HALO, rows_dev)
        tail = rows(jnp.where(block == half - 1, other, main), block, HALO + rows_dev, HALO)
        for line, slot in ((0, main), (2, other)):
            major = lax.div(col_off[slot], side)
            minor = col_off[slot] - major * side
            head = jnp.where(row == line, major.astype(F32), head)
            head = jnp.where(row == line + 1, jnp.where(lane >= minor, 1.0, 0.0), head)
        out[item, 0:window, :] = jnp.concatenate([head, body, tail], axis=0).astype(out.dtype)
        lines = jnp.where(block == storm + 1, bottom, jnp.where(block == storm - 1, top, 0.0))
        out[item, window:, :] = lines.astype(out.dtype)

    for copy in smalls:
        copy.wait()
    for slot in range(2):
        live = counts[0] > slot

        @pl.when(live)
        def _():
            gusts[slot, :, window : window + HALO, :] = jnp.zeros((parts, HALO, LANES), F32)
            one_hot = spread(side)
            for field in range(2):
                for copy in fetch(slot, field):
                    copy.wait()
                both = jnp.concatenate([loaded[slot, field, c, 0:side, :] for c in range(parts)], axis=1)
                both = select_columns(both, one_hot)
                for c in range(parts):
                    loaded[slot, field, c, 0:side, :] = both[:, c * LANES : (c + 1) * LANES]
            advance_into(
                loaded.at[slot],
                coeffs[slot, 0],
                coeffs[slot, 1],
                (buf_a, buf_b),
                gusts.at[slot],
                window + lax.rem(row_off[slot], HALO),
                side,
            )
            body = slice(window, window + side + HALO)
            both = jnp.concatenate([gusts[slot, c, body, :] for c in range(parts)], axis=1).astype(BF16)
            both = jnp.dot(both, gather_turned(side, lax.rem(col_off[slot], side)), preferred_element_type=F32)
            for c in range(parts):
                gusts[slot, c, body, :] = both[:, c * LANES : (c + 1) * LANES]

        @pl.when(jnp.logical_not(live))
        def _():
            gusts[slot, :, window : window + side, :] = jnp.zeros((parts, side, LANES), F32)

    def folded(lines):
        lines = lines.astype(F32)
        return jnp.concatenate([lines[:, at : at + side] for at in range(0, lines.shape[1], side)], axis=0)

    top, bottom = folded(edges[0, 0:PASSES, :]), folded(edges[1, HALO - PASSES : HALO, :])
    for item, (a, b) in enumerate(hops):
        build(own, item, storm ^ jnp.where(tile == 0, a, b))
        build(give, item, storm ^ jnp.where(tile == 0, b, a))


def make_slabs(patches, coeffs, row_off, col_off, counts, classes, hops):
    side = patches.shape[3]
    parts = side // LANES
    rows_dev, cols_dev = classes.shape
    window = rows_dev + 2 * HALO
    hbm = pl.BlockSpec(memory_space=pltpu.HBM)
    vmem = pl.BlockSpec(memory_space=pltpu.VMEM)
    result = jax.ShapeDtypeStruct((len(hops), window + PASSES * cols_dev // side, side), BF16)
    return pl.pallas_call(
        functools.partial(slabs_kernel, hops, rows_dev),
        name="slabs",
        out_shape=(result, result),
        compiler_params=SMALL,
        in_specs=[pl.BlockSpec(memory_space=pltpu.SMEM)] + [hbm] * 5,
        out_specs=(vmem, vmem),
        scratch_shapes=[
            pltpu.SMEM(row_off.shape, row_off.dtype),
            pltpu.SMEM(col_off.shape, col_off.dtype),
            pltpu.SMEM(coeffs.shape, coeffs.dtype),
            pltpu.VMEM((2, 2, parts, side + side // HALO + HALO, LANES), F32),
            pltpu.VMEM((2, side // HALO + 3, HALO, side), F32),
            pltpu.VMEM((2, side // HALO + 3, HALO, side), F32),
            pltpu.VMEM((2, parts, side + 2 * window + HALO, LANES), F32),
            pltpu.VMEM((2, HALO, cols_dev), classes.dtype),
            pltpu.SemaphoreType.DMA((2, 2, parts)),
            pltpu.SemaphoreType.DMA((5,)),
        ],
        cost_estimate=pl.CostEstimate(flops=40 * STEPS * patches.size // 2, bytes_accessed=2 * patches.size, transcendentals=0),
    )(counts, *(pltpu.with_memory_space_constraint(x, pltpu.HBM) for x in (row_off, col_off, coeffs, classes, patches)))


def stamp_kernel(cols_dev, window, hops, *refs):
    arrived, (keep, give, strip) = refs[: len(hops)], refs[len(hops) :]
    items = [ref.at[part] for ref in arrived for part in range(ref.shape[0])]
    side = arrived[0].shape[2]
    strip[...] = jnp.zeros_like(strip)
    storm, tile = lax.axis_index("storm"), lax.axis_index("tile")
    storms = lax.axis_size("storm")
    upper_edge = storm == storms // 2 - 1
    lower_edge = storm == storms // 2
    tail_row = window - HALO
    cut = cols_dev + 2 * LANES

    def put(at, rows, value, mask):
        zero = jnp.zeros_like(value)
        col = pl.multiple_of(LANES + at * side, LANES)
        lo = (slice(rows, rows + value.shape[0]), pl.ds(col, side))
        hi = (slice(rows, rows + value.shape[0]), pl.ds(pl.multiple_of(col + side, LANES), side))
        strip[lo] = jnp.maximum(strip[lo], jnp.where(mask, value, zero))
        strip[hi] = jnp.maximum(strip[hi], jnp.where(mask, zero, value))

    count = len(items)

    def column(item, at):
        return items[item][0:16, 0:LANES].astype(F32)[at, 0].astype(jnp.int32)

    columns = [column(item, 0) for item in range(count)]
    for item in range(count):
        slab = items[item][0:window, :].astype(F32)
        head, body, tail = slab[0:HALO], slab[HALO:tail_row], slab[tail_row:]
        head = jnp.where(lower_edge, 0.0, head)
        tail = jnp.where(upper_edge, 0.0, tail)
        mask = slab[1:2, :] > 0.5
        put(columns[item], 0, jnp.concatenate([head, body, tail], axis=0), mask)

    def other(rows):
        columns = [column(item, 2) for item in range(count)]
        for item in range(count):
            mask = items[item][0:HALO, :].astype(F32)[3:4, :] > 0.5
            put(columns[item], rows, items[item][rows : rows + HALO, :].astype(F32), mask)

    pl.when(lower_edge)(lambda: other(0))
    pl.when(upper_edge)(lambda: other(tail_row))

    for item, (a, b) in enumerate(hops):
        source = storm ^ jnp.where(tile == 0, a, b)

        def lines(to):
            for part in range(arrived[item].shape[0]):
                values = arrived[item][part, window:, :].astype(F32)
                for fold in range(cols_dev // side):
                    at = LANES + jnp.where(tile == part, 0, cols_dev) + fold * side
                    at = pl.ds(pl.multiple_of(at, LANES), side)
                    strip[to : to + PASSES, at] = values[fold * PASSES : (fold + 1) * PASSES]

        pl.when(source == storm - 1)(lambda: lines(window + HALO - PASSES))
        pl.when(source == storm + 1)(lambda: lines(window + HALO))

    own = pl.multiple_of(tile * cols_dev, LANES)
    away = pl.multiple_of((1 - tile) * cols_dev, LANES)
    keep[...] = strip[:, pl.ds(own, cut)].astype(keep.dtype)
    give[...] = strip[:, pl.ds(away, cut)].astype(give.dtype)


def stamp(arrived, hops, rows_dev, cols_dev, map_cols):
    side = arrived[0].shape[2]
    window = rows_dev + 2 * HALO
    height = window + 2 * HALO
    cut = cols_dev + 2 * LANES
    vmem = pl.BlockSpec(memory_space=pltpu.VMEM)
    return pl.pallas_call(
        functools.partial(stamp_kernel, cols_dev, window, hops),
        name="stamp",
        compiler_params=SMALL,
        out_shape=(jax.ShapeDtypeStruct((height, cut), BF16), jax.ShapeDtypeStruct((height, cut), BF16)),
        in_specs=[vmem] * len(arrived),
        out_specs=(vmem, vmem),
        scratch_shapes=[pltpu.VMEM((height, map_cols + 2 * LANES + side), F32)],
    )(*arrived)


def quarter_weight(ids, roughness):
    weights = jnp.full(ids.shape, roughness[0])
    for level in range(1, CLASSES):
        weights = jnp.where(ids == float(level), roughness[level], weights)
    return 0.25 * weights


def blend_kernel(roughness, classes, beside, share):
    rows_dev, cols_dev = classes.shape
    left = lax.axis_index("tile") == 0
    for at in range(0, rows_dev, HALO):
        rows = slice(at, at + HALO)
        near = quarter_weight(beside[rows, :].astype(F32), roughness)
        share[rows, 0:LANES] = jnp.where(left, 0.0, near)
        share[rows, LANES + cols_dev :] = jnp.where(left, near, 0.0)
        share[rows, LANES : LANES + cols_dev] = quarter_weight(classes[rows, :].astype(F32), roughness)


def smooth_kernel(roughness, keep, got, inner, out, share, buf_a, buf_b, done, sems):
    rows_dev, cols_dev = out.shape
    window, cut = share.shape
    left = lax.axis_index("tile") == 0
    storm = lax.axis_index("storm")
    lane = lax.broadcasted_iota(jnp.int32, (HALO, cut), 1)
    within = (lane >= jnp.where(left, LANES, 0)) & (lane < jnp.where(left, cut, LANES + cols_dev))
    lines = jnp.maximum(keep[window:, :], got[window:, :]).astype(F32)
    for at, line, inside in (
        (0, 0, storm > 0),
        (window - HALO, HALO, storm < lax.axis_size("storm") - 1),
    ):
        weights = quarter_weight(lines[line : line + HALO], roughness)
        share[at : at + HALO, :] = jnp.where(within, jnp.where(inside, weights, 0.0), 0.0)
    share[HALO : HALO + rows_dev, :] = inner[...]
    pad = HALO
    chunk = 8
    bufs = (buf_a, buf_b)
    for buf in bufs:
        buf[0:pad, :] = jnp.zeros((pad, cut), F32)
        buf[pad + window :, :] = jnp.zeros((pad, cut), F32)
    buf_a[pad : pad + window, :] = jnp.maximum(keep[0:window, :], got[0:window, :]).astype(F32)
    sends = []
    for step in range(PASSES):
        src, dst = bufs[step % 2], bufs[(step + 1) % 2]
        final = step + 1 == PASSES
        for row in range(HALO if final else 0, window - HALO if final else window, chunk):
            at = pad + row
            v = src[at : at + chunk, :]
            around = (
                src[at - 1 : at - 1 + chunk, :]
                + src[at + 1 : at + 1 + chunk, :]
                + pltpu.roll(v, 1, 1)
                + pltpu.roll(v, cut - 1, 1)
            )
            w = share[row : row + chunk, :]
            new = v - 4.0 * w * v + w * around
            if final:
                to = row - HALO
                done[to : to + chunk, :] = new[:, LANES : LANES + cols_dev]
                if (to + chunk) % SEND_ROWS == 0:
                    part = pl.ds(to + chunk - SEND_ROWS, SEND_ROWS)
                    sends.append(pltpu.make_async_copy(done.at[part], out.at[part], sems.at[to // SEND_ROWS]))
                    sends[-1].start()
            else:
                dst[at : at + chunk, :] = jnp.where(w > 0.0, new, 0.0)
    for send in sends:
        send.wait()


FAR_FIRST = ((10, 11), (9, 1), (12, 13), (15, 2), (5, 7), (3, 4), (6, 8), (0, 14))


def routes(storms):
    group = 2 * len(FAR_FIRST)
    if storms % group:
        return [(k, k + storms // 2) for k in range(storms // 2)]
    return [(base + a, base + b) for base in range(0, storms, group) for a, b in FAR_FIRST]


def window_map(patches, patch_coeffs, row_offset, col_offset, live_counts, class_map, roughness):
    storms = lax.axis_size("storm")
    rows_dev, cols_dev = class_map.shape
    tiles = lax.axis_size("tile")
    map_cols = cols_dev * tiles
    smem = pl.BlockSpec(memory_space=pltpu.SMEM)
    vmem = pl.BlockSpec(memory_space=pltpu.VMEM)
    window = rows_dev + 2 * HALO
    cut = cols_dev + 2 * LANES
    t = lax.axis_index("tile")
    swap = [(0, 1), (1, 0)]
    hops = routes(storms)

    own, give = make_slabs(patches, patch_coeffs, row_offset, col_offset, live_counts, class_map, hops)
    both = jnp.stack([own, lax.ppermute(give, "tile", swap)], axis=1)
    both, ids = lax.optimization_barrier((both, class_map))
    items = []
    for item, (a, b) in enumerate(hops):
        pairs = [(2 * i + j, 2 * (i ^ k) + j) for i in range(storms) for j, k in enumerate((a, b))]
        items.append(lax.ppermute(both[item], ("storm", "tile"), pairs))

    edge = lax.dynamic_slice_in_dim(ids, jnp.where(t == 0, cols_dev - LANES, 0), LANES, 1).astype(BF16)
    beside = lax.ppermute(edge, "tile", swap)
    share = pl.pallas_call(
        blend_kernel,
        name="blend",
        compiler_params=SMALL,
        out_shape=jax.ShapeDtypeStruct((rows_dev, cut), F32),
        in_specs=[smem, vmem, vmem],
        out_specs=vmem,
    )(roughness, class_map, beside)

    *items, share = lax.optimization_barrier((*items, share))
    keep, give = stamp(items, hops, rows_dev, cols_dev, map_cols)
    got = lax.ppermute(give, "tile", swap)
    return pl.pallas_call(
        smooth_kernel,
        name="smooth",
        compiler_params=SMALL,
        out_shape=jax.ShapeDtypeStruct((rows_dev, cols_dev), F32),
        in_specs=[smem, vmem, vmem, vmem],
        out_specs=pl.BlockSpec(memory_space=pl.ANY),
        scratch_shapes=[
            pltpu.VMEM((window, cut), F32),
            pltpu.VMEM((window + 2 * HALO, cut), F32),
            pltpu.VMEM((window + 2 * HALO, cut), F32),
            pltpu.VMEM((rows_dev, cols_dev), F32),
            pltpu.SemaphoreType.DMA((rows_dev // SEND_ROWS,)),
        ],
    )(roughness, keep, got, share)


def solution(mesh):
    return jax.shard_map(
        window_map,
        mesh=mesh,
        in_specs=(
            P(("grp", "storm", "tile"), None, None, None),
            P(("grp", "storm", "tile"), None),
            P(("grp", "storm", "tile")),
            P(("grp", "storm", "tile")),
            P(("grp", "storm", "tile")),
            P(("grp", "storm"), "tile"),
            P(),
        ),
        out_specs=P(("grp", "storm"), "tile"),
        check_vma=False,
    )
```

time: 39.6 us -> 42 us (1.061)
  the two profiles are of different devices: /device:TPU:17 before, /device:TPU:0 now
where the time goes in v1:
time: 42 us; the launch traced here: 41.8 us
  starting transfers between devices  24.9 us (59%)
  waiting for transfers between devices  10.7 us (25%)
  Pallas kernels  5.31 us (13%)
  between operations  0.74 us (2%)
    ppermute x8, starting transfers between devices, window_map(): items.append(lax.ppermute(both[item], ('storm', 'tile'), pairs))  22.2 us
    ppermute x8, waiting for transfers between devices, window_map(): items.append(lax.ppermute(both[item], ('storm', 'tile'), pairs))  7.83 us
    pallas_call x1, Pallas kernels, window_map(): pl.pallas_call(smooth_kernel, name='smooth', compiler_params=SMALL, out_s...  2.54 us
    ppermute x1, starting transfers between devices, window_map(): beside = lax.ppermute(edge, 'tile', swap)  2.1 us
    ppermute x1, waiting for transfers between devices, window_map(): got = lax.ppermute(give, 'tile', swap)  1.5 us
    ppermute x1, waiting for transfers between devices, window_map(): both = jnp.stack([own, lax.ppermute(give, 'tile', swap)], axis=1)  1.35 us
    pallas_call x1, Pallas kernels, make_slabs(): pl.pallas_call(functools.partial(slabs_kernel, hops, rows_dev), name='sla...  1.35 us
    pallas_call x1, Pallas kernels, window_map(): pl.pallas_call(blend_kernel, name='blend', compiler_params=SMALL, out_sha...  0.86 us
  transfers between devices with their start and end apart: 11, of which 5 were waited for; matrix products, arithmetic and copies ran while one was open for 0% of the time, Pallas kernels for 2%

profile of v1, /device:TPU:0, one launch (start us, length us, event | category | flops | bytes accessed | tf_op | source)
XLA Modules:
  0.0 41.8 jit_solution(3699967538675590455)
XLA Ops:
  0.7 1.3 %slabs.1 = (bf16[8,96,256]{2,1,0:T(8,128)(2,1)S(1)}, bf16[8,96,256]{2,1,0:T(8,128)(2,1)S(1)}) custom-call(s32[1]{0:T(128)S(6)} %copy.8.counts, s32[2]{0:T(128)} %row_hbm.1, s32[2]{0:T(128)} %col_hbm.1, f32[2,2]{1,0:T(2,128)} %coeffs_hbm.1, s32[64,1024]{1,0:T(8,128)} %classes.3, f32[2,2,256,256]{3,2,1,0:T(8,128)} %patches.1), custom_call_target="tpu_custom_call" | custom-call | flops 31457280 | bytes 524288 | tf_op jit(solution)/shard_map/slabs/pallas_call | solution.py:243
  2.0 0.6 %collective-permute-start = (bf16[8,96,256]{2,1,0:T(8,128)(2,1)S(1)}, bf16[8,96,256]{2,1,0:T(8,128)(2,1)S(1)}, u32[]{:S(2)}, u32[]{:S(2)}) collective-permute-start(bf16[8,96,256]{2,1,0:T(8,128)(2,1)S(1)} %get-tuple-element.21), channel_id=1, source_target_pairs={{0,1},{1,0},{2,3},{3,2},{4,5},{5,4},{6,7},{7,6},{8,9},{9,8},{10,11... | collective-permute-start | bytes 1179656 | tf_op jit(solution)/shard_map/ppermute | solution.py:438
  2.6 1.3 %collective-permute-done = bf16[8,96,256]{2,1,0:T(8,128)(2,1)S(1)} collective-permute-done((bf16[8,96,256]{2,1,0:T(8,128)(2,1)S(1)}, bf16[8,96,256]{2,1,0:T(8,128)(2,1)S(1)}, u32[]{:S(2)}, u32[]{:S(2)}) %collective-permute-start) | collective-permute-done | bytes 393248 | tf_op jit(solution)/shard_map/ppermute | solution.py:438
  3.9 0.1 pad_maximum_fusion
  4.0 0.0 copy-start
  4.0 0.1 slice_bitcast_fusion
  4.1 0.7 %collective-permute-start.8 = (bf16[2,96,256]{2,1,0:T(8,128)(2,1)S(1)}, bf16[2,96,256]{2,1,0:T(8,128)(2,1)S(1)}, u32[]{:S(2)}, u32[]{:S(2)}) collective-permute-start(bf16[2,96,256]{2,1,0:T(8,128)(2,1)S(1)} %get-tuple-element.35), channel_id=1, source_target_pairs={{0,0},{1,29},{2,2},{3,31},{4,4},{5,25},{6,6},{7,27},{8,8},{9,21},{... | collective-permute-start | bytes 294920 | tf_op jit(solution)/shard_map/ppermute | solution.py:443
  4.7 6.6 %collective-permute-start.7 = (bf16[2,96,256]{2,1,0:T(8,128)(2,1)S(1)}, bf16[2,96,256]{2,1,0:T(8,128)(2,1)S(1)}, u32[]{:S(2)}, u32[]{:S(2)}) collective-permute-start(bf16[2,96,256]{2,1,0:T(8,128)(2,1)S(1)} %get-tuple-element.36), channel_id=1, source_target_pairs={{0,12},{1,17},{2,14},{3,19},{4,8},{5,21},{6,10},{7,23},{8,4},{9,25... | collective-permute-start | bytes 294920 | tf_op jit(solution)/shard_map/ppermute | solution.py:443
  11.3 3.4 %collective-permute-start.6 = (bf16[2,96,256]{2,1,0:T(8,128)(2,1)S(1)}, bf16[2,96,256]{2,1,0:T(8,128)(2,1)S(1)}, u32[]{:S(2)}, u32[]{:S(2)}) collective-permute-start(bf16[2,96,256]{2,1,0:T(8,128)(2,1)S(1)} %get-tuple-element.37), channel_id=1, source_target_pairs={{0,6},{1,9},{2,4},{3,11},{4,2},{5,13},{6,0},{7,15},{8,14},{9,1},{1... | collective-permute-start | bytes 294920 | tf_op jit(solution)/shard_map/ppermute | solution.py:443
  14.8 2.1 %collective-permute-start.9 = (bf16[64,128]{1,0:T(8,128)(2,1)S(1)}, bf16[64,128]{1,0:T(8,128)(2,1)S(1)}, u32[]{:S(2)}, u32[]{:S(2)}) collective-permute-start(bf16[64,128]{1,0:T(8,128)(2,1)S(1)} %dynamic-slice_convert_fusion), channel_id=1, source_target_pairs={{0,1},{1,0},{2,3},{3,2},{4,5},{5,4},{6,7},{7,6},{8,9},{9,8},{10,11... | collective-permute-start | bytes 49160 | tf_op jit(solution)/shard_map/ppermute | solution.py:446
  16.9 2.9 %collective-permute-start.5 = (bf16[2,96,256]{2,1,0:T(8,128)(2,1)S(1)}, bf16[2,96,256]{2,1,0:T(8,128)(2,1)S(1)}, u32[]{:S(2)}, u32[]{:S(2)}) collective-permute-start(bf16[2,96,256]{2,1,0:T(8,128)(2,1)S(1)} %get-tuple-element.38), channel_id=1, source_target_pairs={{0,10},{1,15},{2,8},{3,13},{4,14},{5,11},{6,12},{7,9},{8,2},{9,7},... | collective-permute-start | bytes 294920 | tf_op jit(solution)/shard_map/ppermute | solution.py:443
  19.8 0.0 collective-permute-done.9.beside
  19.8 2.8 %collective-permute-start.4 = (bf16[2,96,256]{2,1,0:T(8,128)(2,1)S(1)}, bf16[2,96,256]{2,1,0:T(8,128)(2,1)S(1)}, u32[]{:S(2)}, u32[]{:S(2)}) collective-permute-start(bf16[2,96,256]{2,1,0:T(8,128)(2,1)S(1)} %get-tuple-element.39), channel_id=1, source_target_pairs={{0,30},{1,5},{2,28},{3,7},{4,26},{5,1},{6,24},{7,3},{8,22},{9,13},... | collective-permute-start | bytes 294920 | tf_op jit(solution)/shard_map/ppermute | solution.py:443
  22.6 1.0 %collective-permute-start.3 = (bf16[2,96,256]{2,1,0:T(8,128)(2,1)S(1)}, bf16[2,96,256]{2,1,0:T(8,128)(2,1)S(1)}, u32[]{:S(2)}, u32[]{:S(2)}) collective-permute-start(bf16[2,96,256]{2,1,0:T(8,128)(2,1)S(1)} %get-tuple-element.40), channel_id=1, source_target_pairs={{0,24},{1,27},{2,26},{3,25},{4,28},{5,31},{6,30},{7,29},{8,16},{9,... | collective-permute-start | bytes 294920 | tf_op jit(solution)/shard_map/ppermute | solution.py:443
  23.6 1.7 %collective-permute-start.2 = (bf16[2,96,256]{2,1,0:T(8,128)(2,1)S(1)}, bf16[2,96,256]{2,1,0:T(8,128)(2,1)S(1)}, u32[]{:S(2)}, u32[]{:S(2)}) collective-permute-start(bf16[2,96,256]{2,1,0:T(8,128)(2,1)S(1)} %get-tuple-element.41), channel_id=1, source_target_pairs={{0,18},{1,3},{2,16},{3,1},{4,22},{5,7},{6,20},{7,5},{8,26},{9,11},... | collective-permute-start | bytes 294920 | tf_op jit(solution)/shard_map/ppermute | solution.py:443
  25.3 3.1 %collective-permute-start.1 = (bf16[2,96,256]{2,1,0:T(8,128)(2,1)S(1)}, bf16[2,96,256]{2,1,0:T(8,128)(2,1)S(1)}, u32[]{:S(2)}, u32[]{:S(2)}) collective-permute-start(bf16[2,96,256]{2,1,0:T(8,128)(2,1)S(1)} %get-tuple-element.42), channel_id=1, source_target_pairs={{0,20},{1,23},{2,22},{3,21},{4,16},{5,19},{6,18},{7,17},{8,28},{9,... | collective-permute-start | bytes 294920 | tf_op jit(solution)/shard_map/ppermute | solution.py:443
  28.4 0.9 %blend.1.inner = f32[64,1280]{1,0:T(8,128)S(1)} custom-call(f32[16]{0:T(128)S(1)} %copy-done.1, s32[64,1024]{1,0:T(8,128)S(1)} %copy-done, bf16[64,128]{1,0:T(8,128)(2,1)S(1)} %collective-permute-done.9.beside), custom_call_target="tpu_custom_call" | custom-call | tf_op jit(solution)/shard_map/blend/pallas_call | solution.py:447
  29.3 0.6 %collective-permute-done.3.refs_2_ = bf16[2,96,256]{2,1,0:T(8,128)(2,1)S(1)} collective-permute-done((bf16[2,96,256]{2,1,0:T(8,128)(2,1)S(1)}, bf16[2,96,256]{2,1,0:T(8,128)(2,1)S(1)}, u32[]{:S(2)}, u32[]{:S(2)}) %collective-permute-start.3) | collective-permute-done | bytes 98336 | tf_op jit(solution)/shard_map/ppermute | solution.py:443
  29.9 6.2 %collective-permute-done.2.refs_1_ = bf16[2,96,256]{2,1,0:T(8,128)(2,1)S(1)} collective-permute-done((bf16[2,96,256]{2,1,0:T(8,128)(2,1)S(1)}, bf16[2,96,256]{2,1,0:T(8,128)(2,1)S(1)}, u32[]{:S(2)}, u32[]{:S(2)}) %collective-permute-start.2) | collective-permute-done | bytes 98336 | tf_op jit(solution)/shard_map/ppermute | solution.py:443
  36.1 1.0 %collective-permute-done.1.refs_0_ = bf16[2,96,256]{2,1,0:T(8,128)(2,1)S(1)} collective-permute-done((bf16[2,96,256]{2,1,0:T(8,128)(2,1)S(1)}, bf16[2,96,256]{2,1,0:T(8,128)(2,1)S(1)}, u32[]{:S(2)}, u32[]{:S(2)}) %collective-permute-start.1) | collective-permute-done | bytes 98336 | tf_op jit(solution)/shard_map/ppermute | solution.py:443
  37.1 0.6 %stamp.1 = (bf16[96,1280]{1,0:T(8,128)(2,1)S(1)}, bf16[96,1280]{1,0:T(8,128)(2,1)S(1)}) custom-call(bf16[2,96,256]{2,1,0:T(8,128)(2,1)S(1)} %collective-permute-done.1.refs_0_, bf16[2,96,256]{2,1,0:T(8,128)(2,1)S(1)} %collective-permute-done.2.refs_1_, bf16[2,96,256]{2,1,0:T(8,128)(2,1)S(1)} %collective-permute-done.3.refs_2_, ...), custom_call_target="tpu_custom_call" | custom-call | tf_op jit(solution)/shard_map/stamp/pallas_call | solution.py:335
  37.7 0.1 collective-permute-start.10
  37.7 1.5 %collective-permute-done.10.got = bf16[96,1280]{1,0:T(8,128)(2,1)S(1)} collective-permute-done((bf16[96,1280]{1,0:T(8,128)(2,1)S(1)}, bf16[96,1280]{1,0:T(8,128)(2,1)S(1)}, u32[]{:S(2)}, u32[]{:S(2)}) %collective-permute-start.10) | collective-permute-done | bytes 245792 | tf_op jit(solution)/shard_map/ppermute | solution.py:458
  39.2 2.5 %smooth.1 = f32[64,1024]{1,0:T(8,128)} custom-call(f32[16]{0:T(128)S(1)} %copy-done.1, bf16[96,1280]{1,0:T(8,128)(2,1)S(1)} %get-tuple-element.32.keep, bf16[96,1280]{1,0:T(8,128)(2,1)S(1)} %collective-permute-done.10.got, f32[64,1280]{1,0:T(8,128)S(1)} %blend.1.inner), custom_call_target="tpu_custom_call" | custom-call | tf_op jit(solution)/shard_map/smooth/pallas_call | solution.py:459
  (9 shorter events, 0.0 us)
Async XLA Ops:
  2.0 1.9 %collective-permute-start = (bf16[8,96,256]{2,1,0:T(8,128)(2,1)S(1)}, bf16[8,96,256]{2,1,0:T(8,128)(2,1)S(1)}, u32[]{:S(2)}, u32[]{:S(2)}) collective-permute-start(bf16[8,96,256]{2,1,0:T(8,128)(2,1)S(1)} %get-tuple-element.21), channel_id=1, source_target_pairs={{0,1},{1,0},{2,3},{3,2},{4,5},{5,4},{6,7},{7,6},{8,9},{9,8},{10,11... | collective-permute-start | bytes 1179656 | tf_op jit(solution)/shard_map/ppermute | solution.py:438
  4.0 10.8 %copy-start = (s32[64,1024]{1,0:T(8,128)S(1)}, s32[64,1024]{1,0:T(8,128)}, u32[]{:S(2)}) copy-start(s32[64,1024]{1,0:T(8,128)} %classes.3) | copy-start | bytes 786436
  4.1 18.5 %collective-permute-start.8 = (bf16[2,96,256]{2,1,0:T(8,128)(2,1)S(1)}, bf16[2,96,256]{2,1,0:T(8,128)(2,1)S(1)}, u32[]{:S(2)}, u32[]{:S(2)}) collective-permute-start(bf16[2,96,256]{2,1,0:T(8,128)(2,1)S(1)} %get-tuple-element.35), channel_id=1, source_target_pairs={{0,0},{1,29},{2,2},{3,31},{4,4},{5,25},{6,6},{7,27},{8,8},{9,21},{... | collective-permute-start | bytes 294920 | tf_op jit(solution)/shard_map/ppermute | solution.py:443
  4.7 18.8 %collective-permute-start.7 = (bf16[2,96,256]{2,1,0:T(8,128)(2,1)S(1)}, bf16[2,96,256]{2,1,0:T(8,128)(2,1)S(1)}, u32[]{:S(2)}, u32[]{:S(2)}) collective-permute-start(bf16[2,96,256]{2,1,0:T(8,128)(2,1)S(1)} %get-tuple-element.36), channel_id=1, source_target_pairs={{0,12},{1,17},{2,14},{3,19},{4,8},{5,21},{6,10},{7,23},{8,4},{9,25... | collective-permute-start | bytes 294920 | tf_op jit(solution)/shard_map/ppermute | solution.py:443
  11.3 13.9 %collective-permute-start.6 = (bf16[2,96,256]{2,1,0:T(8,128)(2,1)S(1)}, bf16[2,96,256]{2,1,0:T(8,128)(2,1)S(1)}, u32[]{:S(2)}, u32[]{:S(2)}) collective-permute-start(bf16[2,96,256]{2,1,0:T(8,128)(2,1)S(1)} %get-tuple-element.37), channel_id=1, source_target_pairs={{0,6},{1,9},{2,4},{3,11},{4,2},{5,13},{6,0},{7,15},{8,14},{9,1},{1... | collective-permute-start | bytes 294920 | tf_op jit(solution)/shard_map/ppermute | solution.py:443
  14.8 5.0 %collective-permute-start.9 = (bf16[64,128]{1,0:T(8,128)(2,1)S(1)}, bf16[64,128]{1,0:T(8,128)(2,1)S(1)}, u32[]{:S(2)}, u32[]{:S(2)}) collective-permute-start(bf16[64,128]{1,0:T(8,128)(2,1)S(1)} %dynamic-slice_convert_fusion), channel_id=1, source_target_pairs={{0,1},{1,0},{2,3},{3,2},{4,5},{5,4},{6,7},{7,6},{8,9},{9,8},{10,11... | collective-permute-start | bytes 49160 | tf_op jit(solution)/shard_map/ppermute | solution.py:446
  16.9 12.4 %collective-permute-start.5 = (bf16[2,96,256]{2,1,0:T(8,128)(2,1)S(1)}, bf16[2,96,256]{2,1,0:T(8,128)(2,1)S(1)}, u32[]{:S(2)}, u32[]{:S(2)}) collective-permute-start(bf16[2,96,256]{2,1,0:T(8,128)(2,1)S(1)} %get-tuple-element.38), channel_id=1, source_target_pairs={{0,10},{1,15},{2,8},{3,13},{4,14},{5,11},{6,12},{7,9},{8,2},{9,7},... | collective-permute-start | bytes 294920 | tf_op jit(solution)/shard_map/ppermute | solution.py:443
  19.8 9.4 %collective-permute-start.4 = (bf16[2,96,256]{2,1,0:T(8,128)(2,1)S(1)}, bf16[2,96,256]{2,1,0:T(8,128)(2,1)S(1)}, u32[]{:S(2)}, u32[]{:S(2)}) collective-permute-start(bf16[2,96,256]{2,1,0:T(8,128)(2,1)S(1)} %get-tuple-element.39), channel_id=1, source_target_pairs={{0,30},{1,5},{2,28},{3,7},{4,26},{5,1},{6,24},{7,3},{8,22},{9,13},... | collective-permute-start | bytes 294920 | tf_op jit(solution)/shard_map/ppermute | solution.py:443
  22.6 7.3 %collective-permute-start.3 = (bf16[2,96,256]{2,1,0:T(8,128)(2,1)S(1)}, bf16[2,96,256]{2,1,0:T(8,128)(2,1)S(1)}, u32[]{:S(2)}, u32[]{:S(2)}) collective-permute-start(bf16[2,96,256]{2,1,0:T(8,128)(2,1)S(1)} %get-tuple-element.40), channel_id=1, source_target_pairs={{0,24},{1,27},{2,26},{3,25},{4,28},{5,31},{6,30},{7,29},{8,16},{9,... | collective-permute-start | bytes 294920 | tf_op jit(solution)/shard_map/ppermute | solution.py:443
  23.6 4.8 %copy-start.1 = (f32[16]{0:T(128)S(1)}, f32[16]{0:T(128)}, u32[]{:S(2)}) copy-start(f32[16]{0:T(128)} %roughness.3) | copy-start | bytes 196
  23.6 12.5 %collective-permute-start.2 = (bf16[2,96,256]{2,1,0:T(8,128)(2,1)S(1)}, bf16[2,96,256]{2,1,0:T(8,128)(2,1)S(1)}, u32[]{:S(2)}, u32[]{:S(2)}) collective-permute-start(bf16[2,96,256]{2,1,0:T(8,128)(2,1)S(1)} %get-tuple-element.41), channel_id=1, source_target_pairs={{0,18},{1,3},{2,16},{3,1},{4,22},{5,7},{6,20},{7,5},{8,26},{9,11},... | collective-permute-start | bytes 294920 | tf_op jit(solution)/shard_map/ppermute | solution.py:443
  25.3 11.8 %collective-permute-start.1 = (bf16[2,96,256]{2,1,0:T(8,128)(2,1)S(1)}, bf16[2,96,256]{2,1,0:T(8,128)(2,1)S(1)}, u32[]{:S(2)}, u32[]{:S(2)}) collective-permute-start(bf16[2,96,256]{2,1,0:T(8,128)(2,1)S(1)} %get-tuple-element.42), channel_id=1, source_target_pairs={{0,20},{1,23},{2,22},{3,21},{4,16},{5,19},{6,18},{7,17},{8,28},{9,... | collective-permute-start | bytes 294920 | tf_op jit(solution)/shard_map/ppermute | solution.py:443
  37.7 1.6 %collective-permute-start.10 = (bf16[96,1280]{1,0:T(8,128)(2,1)S(1)}, bf16[96,1280]{1,0:T(8,128)(2,1)S(1)}, u32[]{:S(2)}, u32[]{:S(2)}) collective-permute-start(bf16[96,1280]{1,0:T(8,128)(2,1)S(1)} %get-tuple-element.33), channel_id=1, source_target_pairs={{0,1},{1,0},{2,3},{3,2},{4,5},{5,4},{6,7},{7,6},{8,9},{9,8},{10,11... | collective-permute-start | bytes 737288 | tf_op jit(solution)/shard_map/ppermute | solution.py:458

commit v2 on v1

--- a/solution.py
+++ b/solution.py
@@ -13,7 +13,6 @@
 PASSES = 4
 HALO = 8
 LANES = 128
-SEND_ROWS = 16
 SMALL = pltpu.CompilerParams(vmem_limit_bytes=16 * 1024 * 1024)
 F32 = jnp.float32
 BF16 = jnp.bfloat16
@@ -350,68 +349,97 @@
     return 0.25 * weights
 
 
-def blend_kernel(roughness, classes, beside, share):
+def blend_kernel(roughness, classes, beside, stay, share):
     rows_dev, cols_dev = classes.shape
     left = lax.axis_index("tile") == 0
+
+    def fill(rows, cols, ids, inside):
+        weights = quarter_weight(ids, roughness)
+        rest = 1.0 - 4.0 * weights
+        if inside is not None:
+            weights, rest = jnp.where(inside, weights, 0.0), jnp.where(inside, rest, 0.0)
+        stay[rows, cols] = rest
+        share[rows, cols] = weights
+
     for at in range(0, rows_dev, HALO):
         rows = slice(at, at + HALO)
-        near = quarter_weight(beside[rows, :].astype(F32), roughness)
-        share[rows, 0:LANES] = jnp.where(left, 0.0, near)
-        share[rows, LANES + cols_dev :] = jnp.where(left, near, 0.0)
-        share[rows, LANES : LANES + cols_dev] = quarter_weight(classes[rows, :].astype(F32), roughness)
-
-
-def smooth_kernel(roughness, keep, got, inner, out, share, buf_a, buf_b, done, sems):
+        near = beside[rows, :].astype(F32)
+        fill(rows, slice(0, LANES), near, jnp.logical_not(left))
+        fill(rows, slice(LANES + cols_dev, 2 * LANES + cols_dev), near, left)
+        fill(rows, slice(LANES, LANES + cols_dev), classes[rows, :].astype(F32), None)
+
+
+def smooth_kernel(roughness, keep, got, stay, share, out, halo, buf_a, buf_b, done, sems):
     rows_dev, cols_dev = out.shape
-    window, cut = share.shape
+    cut = share.shape[1]
+    window = rows_dev + 2 * HALO
     left = lax.axis_index("tile") == 0
     storm = lax.axis_index("storm")
+    bufs = (buf_a, buf_b)
+    for buf in bufs:
+        buf[0:HALO, :] = jnp.zeros((HALO, cut), F32)
+        buf[HALO + window :, :] = jnp.zeros((HALO, cut), F32)
+    buf_a[HALO : HALO + window, :] = jnp.maximum(keep[0:window, :], got[0:window, :]).astype(F32)
     lane = lax.broadcasted_iota(jnp.int32, (HALO, cut), 1)
     within = (lane >= jnp.where(left, LANES, 0)) & (lane < jnp.where(left, cut, LANES + cols_dev))
     lines = jnp.maximum(keep[window:, :], got[window:, :]).astype(F32)
-    for at, line, inside in (
-        (0, 0, storm > 0),
-        (window - HALO, HALO, storm < lax.axis_size("storm") - 1),
-    ):
-        weights = quarter_weight(lines[line : line + HALO], roughness)
-        share[at : at + HALO, :] = jnp.where(within, jnp.where(inside, weights, 0.0), 0.0)
-    share[HALO : HALO + rows_dev, :] = inner[...]
-    pad = HALO
-    chunk = 8
-    bufs = (buf_a, buf_b)
-    for buf in bufs:
-        buf[0:pad, :] = jnp.zeros((pad, cut), F32)
-        buf[pad + window :, :] = jnp.zeros((pad, cut), F32)
-    buf_a[pad : pad + window, :] = jnp.maximum(keep[0:window, :], got[0:window, :]).astype(F32)
+    for at, inside in ((0, storm > 0), (1, storm < lax.axis_size("storm") - 1)):
+        weights = quarter_weight(lines[at * HALO : (at + 1) * HALO], roughness)
+        rest = 1.0 - 4.0 * weights
+        halo[at, 0] = jnp.where(within, jnp.where(inside, rest, 0.0), 0.0)
+        halo[at, 1] = jnp.where(within, jnp.where(inside, weights, 0.0), 0.0)
+
+    def factors(row, count, cols):
+        top, end = max(row, HALO), min(row + count, HALO + rows_dev)
+        both = [[stay[top - HALO : end - HALO, cols]], [share[top - HALO : end - HALO, cols]]]
+        for kind in range(2):
+            if row < HALO:
+                both[kind].insert(0, halo[0, kind, :, cols])
+            if row + count > HALO + rows_dev:
+                both[kind].append(halo[1, kind, :, cols])
+        return [jnp.concatenate(x, axis=0) if len(x) > 1 else x[0] for x in both]
+
     sends = []
+    tiles = [slice(c, c + LANES) for c in range(0, cut, LANES)]
     for step in range(PASSES):
         src, dst = bufs[step % 2], bufs[(step + 1) % 2]
         final = step + 1 == PASSES
-        for row in range(HALO if final else 0, window - HALO if final else window, chunk):
-            at = pad + row
-            v = src[at : at + chunk, :]
-            around = (
-                src[at - 1 : at - 1 + chunk, :]
-                + src[at + 1 : at + 1 + chunk, :]
-                + pltpu.roll(v, 1, 1)
-                + pltpu.roll(v, cut - 1, 1)
-            )
-            w = share[row : row + chunk, :]
-            new = v - 4.0 * w * v + w * around
+        first_row, last_row = (HALO, HALO + rows_dev) if final else (0, window)
+        chunk = (last_row - first_row) // 2
+        one = lax.broadcasted_iota(jnp.int32, (chunk, LANES), 1)
+        for row in range(first_row, last_row, chunk):
+            at = HALO + row
+            middle, right, back = [], [], []
+
+            def load(c):
+                middle.append(src[at : at + chunk, tiles[c]])
+                right.append(pltpu.roll(middle[c], 1, 1))
+                back.append(pltpu.roll(middle[c], LANES - 1, 1))
+
+            load(0)
+            for c, cols in enumerate(tiles):
+                if c + 1 < len(tiles):
+                    load(c + 1)
+                if final and c in (0, len(tiles) - 1):
+                    continue
+                before = jnp.where(one == 0, right[c - 1], right[c]) if c else right[c]
+                after = jnp.where(one == LANES - 1, back[c + 1], back[c]) if c + 1 < len(tiles) else back[c]
+                around = (src[at - 1 : at - 1 + chunk, cols] + src[at + 1 : at + 1 + chunk, cols]) + (before + after)
+                rest, quarter = factors(row, chunk, cols)
+                new = rest * middle[c] + quarter * around
+                if final:
+                    done[row - HALO : row - HALO + chunk, tiles[c - 1]] = new
+                else:
+                    dst[at : at + chunk, cols] = new
             if final:
-                to = row - HALO
-                done[to : to + chunk, :] = new[:, LANES : LANES + cols_dev]
-                if (to + chunk) % SEND_ROWS == 0:
-                    part = pl.ds(to + chunk - SEND_ROWS, SEND_ROWS)
-                    sends.append(pltpu.make_async_copy(done.at[part], out.at[part], sems.at[to // SEND_ROWS]))
-                    sends[-1].start()
-            else:
-                dst[at : at + chunk, :] = jnp.where(w > 0.0, new, 0.0)
+                part = pl.ds(row - HALO, chunk)
+                sends.append(pltpu.make_async_copy(done.at[part], out.at[part], sems.at[len(sends)]))
+                sends[-1].start()
     for send in sends:
         send.wait()
 
 
-FAR_FIRST = ((10, 11), (9, 1), (12, 13), (15, 2), (5, 7), (3, 4), (6, 8), (0, 14))
+FAR_FIRST = ((10, 8), (9, 1), (14, 11), (13, 2), (5, 7), (3, 4), (6, 15), (0, 12))
 
 
 def routes(storms):
@@ -435,25 +463,30 @@
     hops = routes(storms)
 
     own, give = make_slabs(patches, patch_coeffs, row_offset, col_offset, live_counts, class_map, hops)
-    both = jnp.stack([own, lax.ppermute(give, "tile", swap)], axis=1)
-    both, ids = lax.optimization_barrier((both, class_map))
+    cut_at = len(hops) // 2
+    both = []
+    for part in (slice(0, cut_at), slice(cut_at, len(hops))):
+        theirs = lax.ppermute(give[part], "tile", swap)
+        both.append(jnp.stack([own[part], theirs], axis=1))
+    both[0], ids = lax.optimization_barrier((both[0], class_map))
     items = []
     for item, (a, b) in enumerate(hops):
         pairs = [(2 * i + j, 2 * (i ^ k) + j) for i in range(storms) for j, k in enumerate((a, b))]
-        items.append(lax.ppermute(both[item], ("storm", "tile"), pairs))
+        items.append(lax.ppermute(both[item // cut_at][item % cut_at], ("storm", "tile"), pairs))
 
     edge = lax.dynamic_slice_in_dim(ids, jnp.where(t == 0, cols_dev - LANES, 0), LANES, 1).astype(BF16)
     beside = lax.ppermute(edge, "tile", swap)
-    share = pl.pallas_call(
+    factors = jax.ShapeDtypeStruct((rows_dev, cut), F32)
+    stay, share = pl.pallas_call(
         blend_kernel,
         name="blend",
         compiler_params=SMALL,
-        out_shape=jax.ShapeDtypeStruct((rows_dev, cut), F32),
+        out_shape=(factors, factors),
         in_specs=[smem, vmem, vmem],
-        out_specs=vmem,
+        out_specs=(vmem, vmem),
     )(roughness, class_map, beside)
 
-    *items, share = lax.optimization_barrier((*items, share))
+    *items, stay, share = lax.optimization_barrier((*items, stay, share))
     keep, give = stamp(items, hops, rows_dev, cols_dev, map_cols)
     got = lax.ppermute(give, "tile", swap)
     return pl.pallas_call(
@@ -461,16 +494,16 @@
         name="smooth",
         compiler_params=SMALL,
         out_shape=jax.ShapeDtypeStruct((rows_dev, cols_dev), F32),
-        in_specs=[smem, vmem, vmem, vmem],
+        in_specs=[smem, vmem, vmem, vmem, vmem],
         out_specs=pl.BlockSpec(memory_space=pl.ANY),
         scratch_shapes=[
-            pltpu.VMEM((window, cut), F32),
+            pltpu.VMEM((2, 2, HALO, cut), F32),
             pltpu.VMEM((window + 2 * HALO, cut), F32),
             pltpu.VMEM((window + 2 * HALO, cut), F32),
             pltpu.VMEM((rows_dev, cols_dev), F32),
-            pltpu.SemaphoreType.DMA((rows_dev // SEND_ROWS,)),
+            pltpu.SemaphoreType.DMA((2,)),
         ],
-    )(roughness, keep, got, share)
+    )(roughness, keep, got, stay, share)
 
 
 def solution(mesh):

time: 42 us -> 42.9 us (1.021)
  local copies, waits for them, and re-layouts: 0.06 us -> 0.99 us
  waiting for transfers between devices: 10.7 us -> 11.2 us
    ppermute x9 -> x10, starting transfers between devices: 22.7 us -> 19.9 us  [the longest x8 19.3 us: window_map(): lax.ppermute(both[item // cut_at][item % cut_at], ('storm', 'tile'), pairs)]
    ppermute x1, starting transfers between devices: 2.1 us -> 4.55 us  [window_map(): beside = lax.ppermute(edge, 'tile', swap)]
    unnamed x4, local copies, waits for them, and re-layouts: 0.01 us -> 0.91 us
    ppermute x1, waiting for transfers between devices: 0.01 us -> 0.81 us  [window_map(): beside = lax.ppermute(edge, 'tile', swap)]
    ppermute x9 -> x10, waiting for transfers between devices: 9.18 us -> 8.9 us  [the longest x8 7.95 us: window_map(): lax.ppermute(both[item // cut_at][item % cut_at], ('storm', 'tile'), pairs)]
  transfers between devices with their start and end apart: 11 -> 12, of which waited for: 5 -> 6; matrix products, arithmetic and copies ran while one was open for 0% -> 0% of each run, Pallas kernels for 2% -> 2%
where the time goes in v2:
time: 42.9 us; the launch traced here: 42.6 us
  starting transfers between devices  24.6 us (57%)
  waiting for transfers between devices  11.2 us (26%)
  Pallas kernels  5.05 us (12%)
  local copies, waits for them, and re-layouts  0.99 us (2%)
  between operations  0.76 us (2%)
    ppermute x8, starting transfers between devices, window_map(): lax.ppermute(both[item // cut_at][item % cut_at], ('storm', 'tile'), pairs)  19.3 us
    ppermute x8, waiting for transfers between devices, window_map(): lax.ppermute(both[item // cut_at][item % cut_at], ('storm', 'tile'), pairs)  7.95 us
    ppermute x1, starting transfers between devices, window_map(): beside = lax.ppermute(edge, 'tile', swap)  4.55 us
    pallas_call x1, Pallas kernels, window_map(): pl.pallas_call(smooth_kernel, name='smooth', compiler_params=SMALL, out_s...  2.24 us
    ppermute x1, waiting for transfers between devices, window_map(): got = lax.ppermute(give, 'tile', swap)  1.5 us
    pallas_call x1, Pallas kernels, make_slabs(): pl.pallas_call(functools.partial(slabs_kernel, hops, rows_dev), name='sla...  1.35 us
    ppermute x2, waiting for transfers between devices, window_map(): theirs = lax.ppermute(give[part], 'tile', swap)  0.96 us
    unnamed x4, local copies, waits for them, and re-layouts  0.91 us
  transfers between devices with their start and end apart: 12, of which 6 were waited for; matrix products, arithmetic and copies ran while one was open for 0% of the time, Pallas kernels for 2%

profile of v2, /device:TPU:0, one launch (start us, length us, event | category | flops | bytes accessed | tf_op | source)
XLA Modules:
  0.0 42.6 jit_solution(6614973418095129742)
XLA Ops:
  0.7 1.3 %slabs.1 = (bf16[8,96,256]{2,1,0:T(8,128)(2,1)S(1)}, bf16[8,96,256]{2,1,0:T(8,128)(2,1)S(1)}) custom-call(s32[1]{0:T(128)S(6)} %copy.8.counts, s32[2]{0:T(128)} %row_hbm.1, s32[2]{0:T(128)} %col_hbm.1, f32[2,2]{1,0:T(2,128)} %coeffs_hbm.1, s32[64,1024]{1,0:T(8,128)} %classes.3, f32[2,2,256,256]{3,2,1,0:T(8,128)} %patches.1), custom_call_target="tpu_custom_call" | custom-call | flops 31457280 | bytes 524288 | tf_op jit(solution)/shard_map/slabs/pallas_call | solution.py:242
  2.0 0.6 %collective-permute-start.5 = (bf16[4,96,256]{2,1,0:T(8,128)(2,1)S(1)}, bf16[4,96,256]{2,1,0:T(8,128)(2,1)S(1)}, u32[]{:S(2)}, u32[]{:S(2)}) collective-permute-start(bf16[4,96,256]{2,1,0:T(8,128)(2,1)S(1)} %get-tuple-element.45), channel_id=1, source_target_pairs={{0,1},{1,0},{2,3},{3,2},{4,5},{5,4},{6,7},{7,6},{8,9},{9,8},{10,11... | collective-permute-start | bytes 589832 | tf_op jit(solution)/shard_map/ppermute | solution.py:469
  2.6 0.1 collective-permute-start
  2.7 1.0 %collective-permute-done.5 = bf16[4,96,256]{2,1,0:T(8,128)(2,1)S(1)} collective-permute-done((bf16[4,96,256]{2,1,0:T(8,128)(2,1)S(1)}, bf16[4,96,256]{2,1,0:T(8,128)(2,1)S(1)}, u32[]{:S(2)}, u32[]{:S(2)}) %collective-permute-start.5) | collective-permute-done | bytes 196640 | tf_op jit(solution)/shard_map/ppermute | solution.py:469
  3.7 0.7 %collective-permute-start.9 = (bf16[2,96,256]{2,1,0:T(8,128)(2,1)S(1)}, bf16[2,96,256]{2,1,0:T(8,128)(2,1)S(1)}, u32[]{:S(2)}, u32[]{:S(2)}) collective-permute-start(bf16[2,96,256]{2,1,0:T(8,128)(2,1)S(1)} %get-tuple-element.41), channel_id=1, source_target_pairs={{0,0},{1,25},{2,2},{3,27},{4,4},{5,29},{6,6},{7,31},{8,8},{9,17},{... | collective-permute-start | bytes 294920 | tf_op jit(solution)/shard_map/ppermute | solution.py:475
  4.4 8.6 %collective-permute-start.6 = (bf16[2,96,256]{2,1,0:T(8,128)(2,1)S(1)}, bf16[2,96,256]{2,1,0:T(8,128)(2,1)S(1)}, u32[]{:S(2)}, u32[]{:S(2)}) collective-permute-start(bf16[2,96,256]{2,1,0:T(8,128)(2,1)S(1)} %get-tuple-element.42), channel_id=1, source_target_pairs={{0,10},{1,15},{2,8},{3,13},{4,14},{5,11},{6,12},{7,9},{8,2},{9,7},... | collective-permute-start | bytes 294920 | tf_op jit(solution)/shard_map/ppermute | solution.py:475
  12.9 1.5 %collective-permute-start.8 = (bf16[2,96,256]{2,1,0:T(8,128)(2,1)S(1)}, bf16[2,96,256]{2,1,0:T(8,128)(2,1)S(1)}, u32[]{:S(2)}, u32[]{:S(2)}) collective-permute-start(bf16[2,96,256]{2,1,0:T(8,128)(2,1)S(1)} %get-tuple-element.44), channel_id=1, source_target_pairs={{0,12},{1,31},{2,14},{3,29},{4,8},{5,27},{6,10},{7,25},{8,4},{9,23... | collective-permute-start | bytes 294920 | tf_op jit(solution)/shard_map/ppermute | solution.py:475
  14.5 0.9 %copy-done = s32[64,1024]{1,0:T(8,128)S(1)} copy-done((s32[64,1024]{1,0:T(8,128)S(1)}, s32[64,1024]{1,0:T(8,128)}, u32[]{:S(2)}) %copy-start) | copy-done | bytes 262168
  15.4 4.5 %collective-permute-start.10 = (bf16[64,128]{1,0:T(8,128)(2,1)S(1)}, bf16[64,128]{1,0:T(8,128)(2,1)S(1)}, u32[]{:S(2)}, u32[]{:S(2)}) collective-permute-start(bf16[64,128]{1,0:T(8,128)(2,1)S(1)} %dynamic-slice_convert_fusion), channel_id=1, source_target_pairs={{0,1},{1,0},{2,3},{3,2},{4,5},{5,4},{6,7},{7,6},{8,9},{9,8},{10,11... | collective-permute-start | bytes 49160 | tf_op jit(solution)/shard_map/ppermute | solution.py:478
  20.0 0.8 %collective-permute-done.10.beside = bf16[64,128]{1,0:T(8,128)(2,1)S(1)} collective-permute-done((bf16[64,128]{1,0:T(8,128)(2,1)S(1)}, bf16[64,128]{1,0:T(8,128)(2,1)S(1)}, u32[]{:S(2)}, u32[]{:S(2)}) %collective-permute-start.10) | collective-permute-done | bytes 16416 | tf_op jit(solution)/shard_map/ppermute | solution.py:478
  20.8 4.4 %collective-permute-start.4 = (bf16[2,96,256]{2,1,0:T(8,128)(2,1)S(1)}, bf16[2,96,256]{2,1,0:T(8,128)(2,1)S(1)}, u32[]{:S(2)}, u32[]{:S(2)}) collective-permute-start(bf16[2,96,256]{2,1,0:T(8,128)(2,1)S(1)} %get-tuple-element.49), channel_id=1, source_target_pairs={{0,26},{1,5},{2,24},{3,7},{4,30},{5,1},{6,28},{7,3},{8,18},{9,13},... | collective-permute-start | bytes 294920 | tf_op jit(solution)/shard_map/ppermute | solution.py:475
  25.2 0.0 collective-permute-done.9.refs_7_
  25.2 1.2 %collective-permute-start.3 = (bf16[2,96,256]{2,1,0:T(8,128)(2,1)S(1)}, bf16[2,96,256]{2,1,0:T(8,128)(2,1)S(1)}, u32[]{:S(2)}, u32[]{:S(2)}) collective-permute-start(bf16[2,96,256]{2,1,0:T(8,128)(2,1)S(1)} %get-tuple-element.50), channel_id=1, source_target_pairs={{0,28},{1,23},{2,30},{3,21},{4,24},{5,19},{6,26},{7,17},{8,20},{9,... | collective-permute-start | bytes 294920 | tf_op jit(solution)/shard_map/ppermute | solution.py:475
  26.5 0.0 collective-permute-start.2
  26.5 0.0 collective-permute-done.7.refs_5_
  26.5 2.9 %collective-permute-start.1 = (bf16[2,96,256]{2,1,0:T(8,128)(2,1)S(1)}, bf16[2,96,256]{2,1,0:T(8,128)(2,1)S(1)}, u32[]{:S(2)}, u32[]{:S(2)}) collective-permute-start(bf16[2,96,256]{2,1,0:T(8,128)(2,1)S(1)} %get-tuple-element.52), channel_id=1, source_target_pairs={{0,20},{1,17},{2,22},{3,19},{4,16},{5,21},{6,18},{7,23},{8,28},{9,... | collective-permute-start | bytes 294920 | tf_op jit(solution)/shard_map/ppermute | solution.py:475
  29.4 0.9 %blend.1 = (f32[64,1280]{1,0:T(8,128)S(1)}, f32[64,1280]{1,0:T(8,128)S(1)}) custom-call(f32[16]{0:T(128)S(1)} %copy-done.1, s32[64,1024]{1,0:T(8,128)S(1)} %copy-done, bf16[64,128]{1,0:T(8,128)(2,1)S(1)} %collective-permute-done.10.beside), custom_call_target="tpu_custom_call" | custom-call | tf_op jit(solution)/shard_map/blend/pallas_call | solution.py:480
  30.3 2.9 %collective-permute-done.3.refs_2_ = bf16[2,96,256]{2,1,0:T(8,128)(2,1)S(1)} collective-permute-done((bf16[2,96,256]{2,1,0:T(8,128)(2,1)S(1)}, bf16[2,96,256]{2,1,0:T(8,128)(2,1)S(1)}, u32[]{:S(2)}, u32[]{:S(2)}) %collective-permute-start.3) | collective-permute-done | bytes 98336 | tf_op jit(solution)/shard_map/ppermute | solution.py:475
  33.2 4.1 %collective-permute-done.2.refs_1_ = bf16[2,96,256]{2,1,0:T(8,128)(2,1)S(1)} collective-permute-done((bf16[2,96,256]{2,1,0:T(8,128)(2,1)S(1)}, bf16[2,96,256]{2,1,0:T(8,128)(2,1)S(1)}, u32[]{:S(2)}, u32[]{:S(2)}) %collective-permute-start.2) | collective-permute-done | bytes 98336 | tf_op jit(solution)/shard_map/ppermute | solution.py:475
  37.3 1.0 %collective-permute-done.1.refs_0_ = bf16[2,96,256]{2,1,0:T(8,128)(2,1)S(1)} collective-permute-done((bf16[2,96,256]{2,1,0:T(8,128)(2,1)S(1)}, bf16[2,96,256]{2,1,0:T(8,128)(2,1)S(1)}, u32[]{:S(2)}, u32[]{:S(2)}) %collective-permute-start.1) | collective-permute-done | bytes 98336 | tf_op jit(solution)/shard_map/ppermute | solution.py:475
  38.3 0.6 %stamp.1 = (bf16[96,1280]{1,0:T(8,128)(2,1)S(1)}, bf16[96,1280]{1,0:T(8,128)(2,1)S(1)}) custom-call(bf16[2,96,256]{2,1,0:T(8,128)(2,1)S(1)} %collective-permute-done.1.refs_0_, bf16[2,96,256]{2,1,0:T(8,128)(2,1)S(1)} %collective-permute-done.2.refs_1_, bf16[2,96,256]{2,1,0:T(8,128)(2,1)S(1)} %collective-permute-done.3.refs_2_, ...), custom_call_target="tpu_custom_call" | custom-call | tf_op jit(solution)/shard_map/stamp/pallas_call | solution.py:334
  38.8 0.1 collective-permute-start.11
  38.9 1.5 %collective-permute-done.11.got = bf16[96,1280]{1,0:T(8,128)(2,1)S(1)} collective-permute-done((bf16[96,1280]{1,0:T(8,128)(2,1)S(1)}, bf16[96,1280]{1,0:T(8,128)(2,1)S(1)}, u32[]{:S(2)}, u32[]{:S(2)}) %collective-permute-start.11) | collective-permute-done | bytes 245792 | tf_op jit(solution)/shard_map/ppermute | solution.py:491
  40.4 2.2 %smooth.1 = f32[64,1024]{1,0:T(8,128)} custom-call(f32[16]{0:T(128)S(1)} %copy-done.1, bf16[96,1280]{1,0:T(8,128)(2,1)S(1)} %get-tuple-element.37.keep, bf16[96,1280]{1,0:T(8,128)(2,1)S(1)} %collective-permute-done.11.got, f32[64,1280]{1,0:T(8,128)S(1)} %get-tuple-element.39.stay, f32[64,1280]{1,0:T(8,128)S(1)} %get-tuple-element.40.share), custom_call_target="tpu_custom_call" | custom-call | tf_op jit(solution)/shard_map/smooth/pallas_call | solution.py:492
  (14 shorter events, 0.2 us)
Async XLA Ops:
  2.0 1.6 %collective-permute-start.5 = (bf16[4,96,256]{2,1,0:T(8,128)(2,1)S(1)}, bf16[4,96,256]{2,1,0:T(8,128)(2,1)S(1)}, u32[]{:S(2)}, u32[]{:S(2)}) collective-permute-start(bf16[4,96,256]{2,1,0:T(8,128)(2,1)S(1)} %get-tuple-element.45), channel_id=1, source_target_pairs={{0,1},{1,0},{2,3},{3,2},{4,5},{5,4},{6,7},{7,6},{8,9},{9,8},{10,11... | collective-permute-start | bytes 589832 | tf_op jit(solution)/shard_map/ppermute | solution.py:469
  2.6 11.9 %collective-permute-start = (bf16[4,96,256]{2,1,0:T(8,128)(2,1)S(1)}, bf16[4,96,256]{2,1,0:T(8,128)(2,1)S(1)}, u32[]{:S(2)}, u32[]{:S(2)}) collective-permute-start(bf16[4,96,256]{2,1,0:T(8,128)(2,1)S(1)} %get-tuple-element.46), channel_id=1, source_target_pairs={{0,1},{1,0},{2,3},{3,2},{4,5},{5,4},{6,7},{7,6},{8,9},{9,8},{10,11... | collective-permute-start | bytes 589832 | tf_op jit(solution)/shard_map/ppermute | solution.py:469
  3.7 21.5 %collective-permute-start.9 = (bf16[2,96,256]{2,1,0:T(8,128)(2,1)S(1)}, bf16[2,96,256]{2,1,0:T(8,128)(2,1)S(1)}, u32[]{:S(2)}, u32[]{:S(2)}) collective-permute-start(bf16[2,96,256]{2,1,0:T(8,128)(2,1)S(1)} %get-tuple-element.41), channel_id=1, source_target_pairs={{0,0},{1,25},{2,2},{3,27},{4,4},{5,29},{6,6},{7,31},{8,8},{9,17},{... | collective-permute-start | bytes 294920 | tf_op jit(solution)/shard_map/ppermute | solution.py:475
  4.4 22.1 %collective-permute-start.6 = (bf16[2,96,256]{2,1,0:T(8,128)(2,1)S(1)}, bf16[2,96,256]{2,1,0:T(8,128)(2,1)S(1)}, u32[]{:S(2)}, u32[]{:S(2)}) collective-permute-start(bf16[2,96,256]{2,1,0:T(8,128)(2,1)S(1)} %get-tuple-element.42), channel_id=1, source_target_pairs={{0,10},{1,15},{2,8},{3,13},{4,14},{5,11},{6,12},{7,9},{8,2},{9,7},... | collective-permute-start | bytes 294920 | tf_op jit(solution)/shard_map/ppermute | solution.py:475
  12.9 13.5 %collective-permute-start.7 = (bf16[2,96,256]{2,1,0:T(8,128)(2,1)S(1)}, bf16[2,96,256]{2,1,0:T(8,128)(2,1)S(1)}, u32[]{:S(2)}, u32[]{:S(2)}) collective-permute-start(bf16[2,96,256]{2,1,0:T(8,128)(2,1)S(1)} %get-tuple-element.43), channel_id=1, source_target_pairs={{0,6},{1,9},{2,4},{3,11},{4,2},{5,13},{6,0},{7,15},{8,14},{9,1},{1... | collective-permute-start | bytes 294920 | tf_op jit(solution)/shard_map/ppermute | solution.py:475
  12.9 17.4 %collective-permute-start.8 = (bf16[2,96,256]{2,1,0:T(8,128)(2,1)S(1)}, bf16[2,96,256]{2,1,0:T(8,128)(2,1)S(1)}, u32[]{:S(2)}, u32[]{:S(2)}) collective-permute-start(bf16[2,96,256]{2,1,0:T(8,128)(2,1)S(1)} %get-tuple-element.44), channel_id=1, source_target_pairs={{0,12},{1,31},{2,14},{3,29},{4,8},{5,27},{6,10},{7,25},{8,4},{9,23... | collective-permute-start | bytes 294920 | tf_op jit(solution)/shard_map/ppermute | solution.py:475
  14.5 1.0 %copy-start = (s32[64,1024]{1,0:T(8,128)S(1)}, s32[64,1024]{1,0:T(8,128)}, u32[]{:S(2)}) copy-start(s32[64,1024]{1,0:T(8,128)} %classes.3) | copy-start | bytes 786436
  15.4 5.4 %collective-permute-start.10 = (bf16[64,128]{1,0:T(8,128)(2,1)S(1)}, bf16[64,128]{1,0:T(8,128)(2,1)S(1)}, u32[]{:S(2)}, u32[]{:S(2)}) collective-permute-start(bf16[64,128]{1,0:T(8,128)(2,1)S(1)} %dynamic-slice_convert_fusion), channel_id=1, source_target_pairs={{0,1},{1,0},{2,3},{3,2},{4,5},{5,4},{6,7},{7,6},{8,9},{9,8},{10,11... | collective-permute-start | bytes 49160 | tf_op jit(solution)/shard_map/ppermute | solution.py:478
  20.8 9.5 %collective-permute-start.4 = (bf16[2,96,256]{2,1,0:T(8,128)(2,1)S(1)}, bf16[2,96,256]{2,1,0:T(8,128)(2,1)S(1)}, u32[]{:S(2)}, u32[]{:S(2)}) collective-permute-start(bf16[2,96,256]{2,1,0:T(8,128)(2,1)S(1)} %get-tuple-element.49), channel_id=1, source_target_pairs={{0,26},{1,5},{2,24},{3,7},{4,30},{5,1},{6,28},{7,3},{8,18},{9,13},... | collective-permute-start | bytes 294920 | tf_op jit(solution)/shard_map/ppermute | solution.py:475
  25.2 8.0 %collective-permute-start.3 = (bf16[2,96,256]{2,1,0:T(8,128)(2,1)S(1)}, bf16[2,96,256]{2,1,0:T(8,128)(2,1)S(1)}, u32[]{:S(2)}, u32[]{:S(2)}) collective-permute-start(bf16[2,96,256]{2,1,0:T(8,128)(2,1)S(1)} %get-tuple-element.50), channel_id=1, source_target_pairs={{0,28},{1,23},{2,30},{3,21},{4,24},{5,19},{6,26},{7,17},{8,20},{9,... | collective-permute-start | bytes 294920 | tf_op jit(solution)/shard_map/ppermute | solution.py:475
  26.5 2.9 %copy-start.1 = (f32[16]{0:T(128)S(1)}, f32[16]{0:T(128)}, u32[]{:S(2)}) copy-start(f32[16]{0:T(128)} %roughness.3) | copy-start | bytes 196
  26.5 10.8 %collective-permute-start.2 = (bf16[2,96,256]{2,1,0:T(8,128)(2,1)S(1)}, bf16[2,96,256]{2,1,0:T(8,128)(2,1)S(1)}, u32[]{:S(2)}, u32[]{:S(2)}) collective-permute-start(bf16[2,96,256]{2,1,0:T(8,128)(2,1)S(1)} %get-tuple-element.51), channel_id=1, source_target_pairs={{0,18},{1,3},{2,16},{3,1},{4,22},{5,7},{6,20},{7,5},{8,26},{9,11},... | collective-permute-start | bytes 294920 | tf_op jit(solution)/shard_map/ppermute | solution.py:475
  26.5 11.8 %collective-permute-start.1 = (bf16[2,96,256]{2,1,0:T(8,128)(2,1)S(1)}, bf16[2,96,256]{2,1,0:T(8,128)(2,1)S(1)}, u32[]{:S(2)}, u32[]{:S(2)}) collective-permute-start(bf16[2,96,256]{2,1,0:T(8,128)(2,1)S(1)} %get-tuple-element.52), channel_id=1, source_target_pairs={{0,20},{1,17},{2,22},{3,19},{4,16},{5,21},{6,18},{7,23},{8,28},{9,... | collective-permute-start | bytes 294920 | tf_op jit(solution)/shard_map/ppermute | solution.py:475
  38.8 1.6 %collective-permute-start.11 = (bf16[96,1280]{1,0:T(8,128)(2,1)S(1)}, bf16[96,1280]{1,0:T(8,128)(2,1)S(1)}, u32[]{:S(2)}, u32[]{:S(2)}) collective-permute-start(bf16[96,1280]{1,0:T(8,128)(2,1)S(1)} %get-tuple-element.38), channel_id=1, source_target_pairs={{0,1},{1,0},{2,3},{3,2},{4,5},{5,4},{6,7},{7,6},{8,9},{9,8},{10,11... | collective-permute-start | bytes 737288 | tf_op jit(solution)/shard_map/ppermute | solution.py:491

commit v3 on v2

--- a/solution.py
+++ b/solution.py
@@ -18,27 +18,29 @@
 BF16 = jnp.bfloat16
 
 
+def one_hot(rows):
+    side = rows.shape[1]
+    place = lax.broadcasted_iota(jnp.int32, (side, side), 0)
+    return jnp.where(place == rows, 1.0, 0.0).astype(BF16)
+
+
 def spread(side):
-    column = lax.broadcasted_iota(jnp.int32, (side, side), 0)
-    place = lax.broadcasted_iota(jnp.int32, (side, side), 1)
+    place = lax.broadcasted_iota(jnp.int32, (1, side), 1)
+    return one_hot(side // LANES * lax.rem(place, LANES) + lax.div(place, LANES))
+
+
+def gather_turned(side, turn):
     parts = side // LANES
-    return jnp.where(column == parts * lax.rem(place, LANES) + lax.div(place, LANES), 1.0, 0.0).astype(BF16)
-
-
-def gather_turned(side, turn):
-    place = lax.broadcasted_iota(jnp.int32, (side, side), 0)
-    column = lax.broadcasted_iota(jnp.int32, (side, side), 1)
-    parts = side // LANES
-    moved = parts * lax.rem(place, LANES) + lax.div(place, LANES) + turn
-    moved = jnp.where(moved >= side, moved - side, moved)
-    return jnp.where(column == moved, 1.0, 0.0).astype(BF16)
-
-
-def select_columns(x, one_hot):
+    column = lax.broadcasted_iota(jnp.int32, (1, side), 1) - turn
+    column = jnp.where(column < 0, column + side, column)
+    return one_hot(lax.rem(column, parts) * LANES + lax.div(column, parts))
+
+
+def select_columns(x, places):
     total = None
     for term in range(3):
         piece = x.astype(BF16)
-        product = jnp.dot(piece, one_hot, preferred_element_type=F32)
+        product = jnp.dot(piece, places, preferred_element_type=F32)
         total = product if total is None else total + product
         if term < 2:
             x = x - piece.astype(F32)
@@ -117,6 +119,7 @@
     buf_b,
     gusts,
     edges,
+    hot,
     sems,
     small_sems,
 ):
@@ -186,20 +189,22 @@
         lines = jnp.where(block == storm + 1, bottom, jnp.where(block == storm - 1, top, 0.0))
         out[item, window:, :] = lines.astype(out.dtype)
 
+    hot[2] = spread(side)
     for copy in smalls:
         copy.wait()
     for slot in range(2):
+        hot[slot] = gather_turned(side, lax.rem(col_off[slot], side))
+    for slot in range(2):
         live = counts[0] > slot
 
         @pl.when(live)
         def _():
             gusts[slot, :, window : window + HALO, :] = jnp.zeros((parts, HALO, LANES), F32)
-            one_hot = spread(side)
             for field in range(2):
                 for copy in fetch(slot, field):
                     copy.wait()
                 both = jnp.concatenate([loaded[slot, field, c, 0:side, :] for c in range(parts)], axis=1)
-                both = select_columns(both, one_hot)
+                both = select_columns(both, hot[2])
                 for c in range(parts):
                     loaded[slot, field, c, 0:side, :] = both[:, c * LANES : (c + 1) * LANES]
             advance_into(
@@ -213,7 +218,7 @@
             )
             body = slice(window, window + side + HALO)
             both = jnp.concatenate([gusts[slot, c, body, :] for c in range(parts)], axis=1).astype(BF16)
-            both = jnp.dot(both, gather_turned(side, lax.rem(col_off[slot], side)), preferred_element_type=F32)
+            both = jnp.dot(both, hot[slot], preferred_element_type=F32)
             for c in range(parts):
                 gusts[slot, c, body, :] = both[:, c * LANES : (c + 1) * LANES]
 
@@ -255,6 +260,7 @@
             pltpu.VMEM((2, side // HALO + 3, HALO, side), F32),
             pltpu.VMEM((2, parts, side + 2 * window + HALO, LANES), F32),
             pltpu.VMEM((2, HALO, cols_dev), classes.dtype),
+            pltpu.VMEM((3, side, side), BF16),
             pltpu.SemaphoreType.DMA((2, 2, parts)),
             pltpu.SemaphoreType.DMA((5,)),
         ],
@@ -463,7 +469,7 @@
     hops = routes(storms)
 
     own, give = make_slabs(patches, patch_coeffs, row_offset, col_offset, live_counts, class_map, hops)
-    cut_at = len(hops) // 2
+    cut_at = max(1, len(hops) // 4)
     both = []
     for part in (slice(0, cut_at), slice(cut_at, len(hops))):
         theirs = lax.ppermute(give[part], "tile", swap)
@@ -472,7 +478,8 @@
     items = []
     for item, (a, b) in enumerate(hops):
         pairs = [(2 * i + j, 2 * (i ^ k) + j) for i in range(storms) for j, k in enumerate((a, b))]
-        items.append(lax.ppermute(both[item // cut_at][item % cut_at], ("storm", "tile"), pairs))
+        ready = both[0][item] if item < cut_at else both[1][item - cut_at]
+        items.append(lax.ppermute(ready, ("storm", "tile"), pairs))
 
     edge = lax.dynamic_slice_in_dim(ids, jnp.where(t == 0, cols_dev - LANES, 0), LANES, 1).astype(BF16)
     beside = lax.ppermute(edge, "tile", swap)

time: 42.9 us -> 38.2 us (0.89)
  starting transfers between devices: 24.6 us -> 22.2 us
  waiting for transfers between devices: 11.2 us -> 9.66 us
  local copies, waits for them, and re-layouts: 0.99 us -> 0.16 us
    ppermute x1, starting transfers between devices: 4.55 us -> 2.32 us  [window_map(): beside = lax.ppermute(edge, 'tile', swap)]
    unnamed x4, local copies, waits for them, and re-layouts: 0.91 us -> 0.09 us
    ppermute x1, waiting for transfers between devices: 0.81 us -> 0.01 us  [window_map(): beside = lax.ppermute(edge, 'tile', swap)]
    ppermute x8, waiting for transfers between devices: 7.95 us -> 7.37 us  [window_map(): items.append(lax.ppermute(ready, ('storm', 'tile'), pairs))]
where the time goes in v3:
time: 38.2 us; the launch traced here: 38 us
  starting transfers between devices  22.2 us (58%)
  waiting for transfers between devices  9.66 us (25%)
  Pallas kernels  5.11 us (13%)
  between operations  0.76 us (2%)
    ppermute x8, starting transfers between devices, window_map(): items.append(lax.ppermute(ready, ('storm', 'tile'), pairs))  19.2 us
    ppermute x8, waiting for transfers between devices, window_map(): items.append(lax.ppermute(ready, ('storm', 'tile'), pairs))  7.37 us
    ppermute x1, starting transfers between devices, window_map(): beside = lax.ppermute(edge, 'tile', swap)  2.32 us
    pallas_call x1, Pallas kernels, window_map(): pl.pallas_call(smooth_kernel, name='smooth', compiler_params=SMALL, out_s...  2.24 us
    ppermute x1, waiting for transfers between devices, window_map(): got = lax.ppermute(give, 'tile', swap)  1.5 us
    pallas_call x1, Pallas kernels, make_slabs(): pl.pallas_call(functools.partial(slabs_kernel, hops, rows_dev), name='sla...  1.41 us
    pallas_call x1, Pallas kernels, window_map(): pl.pallas_call(blend_kernel, name='blend', compiler_params=SMALL, out_sha...  0.9 us
    ppermute x2, waiting for transfers between devices, window_map(): theirs = lax.ppermute(give[part], 'tile', swap)  0.79 us
  transfers between devices with their start and end apart: 12, of which 6 were waited for; matrix products, arithmetic and copies ran while one was open for 0% of the time, Pallas kernels for 2%

profile of v3, /device:TPU:0, one launch (start us, length us, event | category | flops | bytes accessed | tf_op | source)
XLA Modules:
  0.0 38.0 jit_solution(13539308230761109860)
XLA Ops:
  0.7 1.4 %slabs.1 = (bf16[8,96,256]{2,1,0:T(8,128)(2,1)S(1)}, bf16[8,96,256]{2,1,0:T(8,128)(2,1)S(1)}) custom-call(s32[1]{0:T(128)S(6)} %copy.8.counts, s32[2]{0:T(128)} %row_hbm.1, s32[2]{0:T(128)} %col_hbm.1, f32[2,2]{1,0:T(2,128)} %coeffs_hbm.1, s32[64,1024]{1,0:T(8,128)} %classes.3, f32[2,2,256,256]{3,2,1,0:T(8,128)} %patches.1), custom_call_target="tpu_custom_call" | custom-call | flops 31457280 | bytes 524288 | tf_op jit(solution)/shard_map/slabs/pallas_call | solution.py:247
  2.1 0.6 %collective-permute-start = (bf16[2,96,256]{2,1,0:T(8,128)(2,1)S(1)}, bf16[2,96,256]{2,1,0:T(8,128)(2,1)S(1)}, u32[]{:S(2)}, u32[]{:S(2)}) collective-permute-start(bf16[2,96,256]{2,1,0:T(8,128)(2,1)S(1)} %slice.37), channel_id=1, source_target_pairs={{0,1},{1,0},{2,3},{3,2},{4,5},{5,4},{6,7},{7,6},{8,9},{9,8},{10,11... | collective-permute-start | bytes 294920 | tf_op jit(solution)/shard_map/ppermute | solution.py:475
  2.7 0.1 collective-permute-start.3
  2.8 0.8 %collective-permute-done = bf16[2,96,256]{2,1,0:T(8,128)(2,1)S(1)} collective-permute-done((bf16[2,96,256]{2,1,0:T(8,128)(2,1)S(1)}, bf16[2,96,256]{2,1,0:T(8,128)(2,1)S(1)}, u32[]{:S(2)}, u32[]{:S(2)}) %collective-permute-start) | collective-permute-done | bytes 98336 | tf_op jit(solution)/shard_map/ppermute | solution.py:475
  3.6 4.9 %collective-permute-start.2 = (bf16[2,96,256]{2,1,0:T(8,128)(2,1)S(1)}, bf16[2,96,256]{2,1,0:T(8,128)(2,1)S(1)}, u32[]{:S(2)}, u32[]{:S(2)}) collective-permute-start(bf16[2,96,256]{2,1,0:T(8,128)(2,1)S(1)} %get-tuple-element.47), channel_id=1, source_target_pairs={{0,18},{1,3},{2,16},{3,1},{4,22},{5,7},{6,20},{7,5},{8,26},{9,11},... | collective-permute-start | bytes 294920 | tf_op jit(solution)/shard_map/ppermute | solution.py:482
  8.6 5.1 %collective-permute-start.1 = (bf16[2,96,256]{2,1,0:T(8,128)(2,1)S(1)}, bf16[2,96,256]{2,1,0:T(8,128)(2,1)S(1)}, u32[]{:S(2)}, u32[]{:S(2)}) collective-permute-start(bf16[2,96,256]{2,1,0:T(8,128)(2,1)S(1)} %get-tuple-element.48), channel_id=1, source_target_pairs={{0,20},{1,17},{2,22},{3,19},{4,16},{5,21},{6,18},{7,23},{8,28},{9,... | collective-permute-start | bytes 294920 | tf_op jit(solution)/shard_map/ppermute | solution.py:482
  13.7 0.1 fusion.10
  13.7 0.8 %collective-permute-start.9 = (bf16[2,96,256]{2,1,0:T(8,128)(2,1)S(1)}, bf16[2,96,256]{2,1,0:T(8,128)(2,1)S(1)}, u32[]{:S(2)}, u32[]{:S(2)}) collective-permute-start(bf16[2,96,256]{2,1,0:T(8,128)(2,1)S(1)} %get-tuple-element.41), channel_id=1, source_target_pairs={{0,0},{1,25},{2,2},{3,27},{4,4},{5,29},{6,6},{7,31},{8,8},{9,17},{... | collective-permute-start | bytes 294920 | tf_op jit(solution)/shard_map/ppermute | solution.py:482
  14.5 0.1 copy-done
  14.6 2.3 %collective-permute-start.10 = (bf16[64,128]{1,0:T(8,128)(2,1)S(1)}, bf16[64,128]{1,0:T(8,128)(2,1)S(1)}, u32[]{:S(2)}, u32[]{:S(2)}) collective-permute-start(bf16[64,128]{1,0:T(8,128)(2,1)S(1)} %dynamic-slice_convert_fusion), channel_id=1, source_target_pairs={{0,1},{1,0},{2,3},{3,2},{4,5},{5,4},{6,7},{7,6},{8,9},{9,8},{10,11... | collective-permute-start | bytes 49160 | tf_op jit(solution)/shard_map/ppermute | solution.py:485
  17.0 3.5 %collective-permute-start.4 = (bf16[2,96,256]{2,1,0:T(8,128)(2,1)S(1)}, bf16[2,96,256]{2,1,0:T(8,128)(2,1)S(1)}, u32[]{:S(2)}, u32[]{:S(2)}) collective-permute-start(bf16[2,96,256]{2,1,0:T(8,128)(2,1)S(1)} %get-tuple-element.42), channel_id=1, source_target_pairs={{0,28},{1,23},{2,30},{3,21},{4,24},{5,19},{6,26},{7,17},{8,20},{9,... | collective-permute-start | bytes 294920 | tf_op jit(solution)/shard_map/ppermute | solution.py:482
  20.4 0.0 collective-permute-done.10.beside
  20.4 1.6 %collective-permute-start.5 = (bf16[2,96,256]{2,1,0:T(8,128)(2,1)S(1)}, bf16[2,96,256]{2,1,0:T(8,128)(2,1)S(1)}, u32[]{:S(2)}, u32[]{:S(2)}) collective-permute-start(bf16[2,96,256]{2,1,0:T(8,128)(2,1)S(1)} %get-tuple-element.43), channel_id=1, source_target_pairs={{0,26},{1,5},{2,24},{3,7},{4,30},{5,1},{6,28},{7,3},{8,18},{9,13},... | collective-permute-start | bytes 294920 | tf_op jit(solution)/shard_map/ppermute | solution.py:482
  22.1 2.9 %collective-permute-done.1.refs_0_ = bf16[2,96,256]{2,1,0:T(8,128)(2,1)S(1)} collective-permute-done((bf16[2,96,256]{2,1,0:T(8,128)(2,1)S(1)}, bf16[2,96,256]{2,1,0:T(8,128)(2,1)S(1)}, u32[]{:S(2)}, u32[]{:S(2)}) %collective-permute-start.1) | collective-permute-done | bytes 98336 | tf_op jit(solution)/shard_map/ppermute | solution.py:482
  25.0 2.1 %collective-permute-start.7 = (bf16[2,96,256]{2,1,0:T(8,128)(2,1)S(1)}, bf16[2,96,256]{2,1,0:T(8,128)(2,1)S(1)}, u32[]{:S(2)}, u32[]{:S(2)}) collective-permute-start(bf16[2,96,256]{2,1,0:T(8,128)(2,1)S(1)} %get-tuple-element.45), channel_id=1, source_target_pairs={{0,6},{1,9},{2,4},{3,11},{4,2},{5,13},{6,0},{7,15},{8,14},{9,1},{1... | collective-permute-start | bytes 294920 | tf_op jit(solution)/shard_map/ppermute | solution.py:482
  27.1 1.2 %collective-permute-start.8 = (bf16[2,96,256]{2,1,0:T(8,128)(2,1)S(1)}, bf16[2,96,256]{2,1,0:T(8,128)(2,1)S(1)}, u32[]{:S(2)}, u32[]{:S(2)}) collective-permute-start(bf16[2,96,256]{2,1,0:T(8,128)(2,1)S(1)} %get-tuple-element.46), channel_id=1, source_target_pairs={{0,12},{1,31},{2,14},{3,29},{4,8},{5,27},{6,10},{7,25},{8,4},{9,23... | collective-permute-start | bytes 294920 | tf_op jit(solution)/shard_map/ppermute | solution.py:482
  28.3 0.9 %blend.1 = (f32[64,1280]{1,0:T(8,128)S(1)}, f32[64,1280]{1,0:T(8,128)S(1)}) custom-call(f32[16]{0:T(128)S(1)} %copy-done.1, s32[64,1024]{1,0:T(8,128)S(1)} %copy-done, bf16[64,128]{1,0:T(8,128)(2,1)S(1)} %collective-permute-done.10.beside), custom_call_target="tpu_custom_call" | custom-call | tf_op jit(solution)/shard_map/blend/pallas_call | solution.py:487
  29.2 0.8 %collective-permute-done.6.refs_4_ = bf16[2,96,256]{2,1,0:T(8,128)(2,1)S(1)} collective-permute-done((bf16[2,96,256]{2,1,0:T(8,128)(2,1)S(1)}, bf16[2,96,256]{2,1,0:T(8,128)(2,1)S(1)}, u32[]{:S(2)}, u32[]{:S(2)}) %collective-permute-start.6) | collective-permute-done | bytes 98336 | tf_op jit(solution)/shard_map/ppermute | solution.py:482
  30.0 2.2 %collective-permute-done.7.refs_5_ = bf16[2,96,256]{2,1,0:T(8,128)(2,1)S(1)} collective-permute-done((bf16[2,96,256]{2,1,0:T(8,128)(2,1)S(1)}, bf16[2,96,256]{2,1,0:T(8,128)(2,1)S(1)}, u32[]{:S(2)}, u32[]{:S(2)}) %collective-permute-start.7) | collective-permute-done | bytes 98336 | tf_op jit(solution)/shard_map/ppermute | solution.py:482
  32.3 1.4 %collective-permute-done.8.refs_6_ = bf16[2,96,256]{2,1,0:T(8,128)(2,1)S(1)} collective-permute-done((bf16[2,96,256]{2,1,0:T(8,128)(2,1)S(1)}, bf16[2,96,256]{2,1,0:T(8,128)(2,1)S(1)}, u32[]{:S(2)}, u32[]{:S(2)}) %collective-permute-start.8) | collective-permute-done | bytes 98336 | tf_op jit(solution)/shard_map/ppermute | solution.py:482
  33.6 0.6 %stamp.1 = (bf16[96,1280]{1,0:T(8,128)(2,1)S(1)}, bf16[96,1280]{1,0:T(8,128)(2,1)S(1)}) custom-call(bf16[2,96,256]{2,1,0:T(8,128)(2,1)S(1)} %collective-permute-done.1.refs_0_, bf16[2,96,256]{2,1,0:T(8,128)(2,1)S(1)} %collective-permute-done.2.refs_1_, bf16[2,96,256]{2,1,0:T(8,128)(2,1)S(1)} %collective-permute-done.4.refs_2_, ...), custom_call_target="tpu_custom_call" | custom-call | tf_op jit(solution)/shard_map/stamp/pallas_call | solution.py:340
  34.2 0.1 collective-permute-start.11
  34.3 1.5 %collective-permute-done.11.got = bf16[96,1280]{1,0:T(8,128)(2,1)S(1)} collective-permute-done((bf16[96,1280]{1,0:T(8,128)(2,1)S(1)}, bf16[96,1280]{1,0:T(8,128)(2,1)S(1)}, u32[]{:S(2)}, u32[]{:S(2)}) %collective-permute-start.11) | collective-permute-done | bytes 245792 | tf_op jit(solution)/shard_map/ppermute | solution.py:498
  35.8 2.2 %smooth.1 = f32[64,1024]{1,0:T(8,128)} custom-call(f32[16]{0:T(128)S(1)} %copy-done.1, bf16[96,1280]{1,0:T(8,128)(2,1)S(1)} %get-tuple-element.37.keep, bf16[96,1280]{1,0:T(8,128)(2,1)S(1)} %collective-permute-done.11.got, f32[64,1280]{1,0:T(8,128)S(1)} %get-tuple-element.39.stay, f32[64,1280]{1,0:T(8,128)S(1)} %get-tuple-element.40.share), custom_call_target="tpu_custom_call" | custom-call | tf_op jit(solution)/shard_map/smooth/pallas_call | solution.py:499
  (16 shorter events, 0.1 us)
Async XLA Ops:
  2.1 1.5 %collective-permute-start = (bf16[2,96,256]{2,1,0:T(8,128)(2,1)S(1)}, bf16[2,96,256]{2,1,0:T(8,128)(2,1)S(1)}, u32[]{:S(2)}, u32[]{:S(2)}) collective-permute-start(bf16[2,96,256]{2,1,0:T(8,128)(2,1)S(1)} %slice.37), channel_id=1, source_target_pairs={{0,1},{1,0},{2,3},{3,2},{4,5},{5,4},{6,7},{7,6},{8,9},{9,8},{10,11... | collective-permute-start | bytes 294920 | tf_op jit(solution)/shard_map/ppermute | solution.py:475
  2.7 11.0 %collective-permute-start.3 = (bf16[6,96,256]{2,1,0:T(8,128)(2,1)S(1)}, bf16[6,96,256]{2,1,0:T(8,128)(2,1)S(1)}, u32[]{:S(2)}, u32[]{:S(2)}) collective-permute-start(bf16[6,96,256]{2,1,0:T(8,128)(2,1)S(1)} %slice.41), channel_id=1, source_target_pairs={{0,1},{1,0},{2,3},{3,2},{4,5},{5,4},{6,7},{7,6},{8,9},{9,8},{10,11... | collective-permute-start | bytes 884744 | tf_op jit(solution)/shard_map/ppermute | solution.py:475
  3.6 18.4 %collective-permute-start.2 = (bf16[2,96,256]{2,1,0:T(8,128)(2,1)S(1)}, bf16[2,96,256]{2,1,0:T(8,128)(2,1)S(1)}, u32[]{:S(2)}, u32[]{:S(2)}) collective-permute-start(bf16[2,96,256]{2,1,0:T(8,128)(2,1)S(1)} %get-tuple-element.47), channel_id=1, source_target_pairs={{0,18},{1,3},{2,16},{3,1},{4,22},{5,7},{6,20},{7,5},{8,26},{9,11},... | collective-permute-start | bytes 294920 | tf_op jit(solution)/shard_map/ppermute | solution.py:482
  8.6 16.4 %collective-permute-start.1 = (bf16[2,96,256]{2,1,0:T(8,128)(2,1)S(1)}, bf16[2,96,256]{2,1,0:T(8,128)(2,1)S(1)}, u32[]{:S(2)}, u32[]{:S(2)}) collective-permute-start(bf16[2,96,256]{2,1,0:T(8,128)(2,1)S(1)} %get-tuple-element.48), channel_id=1, source_target_pairs={{0,20},{1,17},{2,22},{3,19},{4,16},{5,21},{6,18},{7,23},{8,28},{9,... | collective-permute-start | bytes 294920 | tf_op jit(solution)/shard_map/ppermute | solution.py:482
  13.7 1.0 %copy-start = (s32[64,1024]{1,0:T(8,128)S(1)}, s32[64,1024]{1,0:T(8,128)}, u32[]{:S(2)}) copy-start(s32[64,1024]{1,0:T(8,128)} %classes.3) | copy-start | bytes 786436
  13.7 13.3 %collective-permute-start.9 = (bf16[2,96,256]{2,1,0:T(8,128)(2,1)S(1)}, bf16[2,96,256]{2,1,0:T(8,128)(2,1)S(1)}, u32[]{:S(2)}, u32[]{:S(2)}) collective-permute-start(bf16[2,96,256]{2,1,0:T(8,128)(2,1)S(1)} %get-tuple-element.41), channel_id=1, source_target_pairs={{0,0},{1,25},{2,2},{3,27},{4,4},{5,29},{6,6},{7,31},{8,8},{9,17},{... | collective-permute-start | bytes 294920 | tf_op jit(solution)/shard_map/ppermute | solution.py:482
  14.6 5.8 %collective-permute-start.10 = (bf16[64,128]{1,0:T(8,128)(2,1)S(1)}, bf16[64,128]{1,0:T(8,128)(2,1)S(1)}, u32[]{:S(2)}, u32[]{:S(2)}) collective-permute-start(bf16[64,128]{1,0:T(8,128)(2,1)S(1)} %dynamic-slice_convert_fusion), channel_id=1, source_target_pairs={{0,1},{1,0},{2,3},{3,2},{4,5},{5,4},{6,7},{7,6},{8,9},{9,8},{10,11... | collective-permute-start | bytes 49160 | tf_op jit(solution)/shard_map/ppermute | solution.py:485
  17.0 12.2 %collective-permute-start.4 = (bf16[2,96,256]{2,1,0:T(8,128)(2,1)S(1)}, bf16[2,96,256]{2,1,0:T(8,128)(2,1)S(1)}, u32[]{:S(2)}, u32[]{:S(2)}) collective-permute-start(bf16[2,96,256]{2,1,0:T(8,128)(2,1)S(1)} %get-tuple-element.42), channel_id=1, source_target_pairs={{0,28},{1,23},{2,30},{3,21},{4,24},{5,19},{6,26},{7,17},{8,20},{9,... | collective-permute-start | bytes 294920 | tf_op jit(solution)/shard_map/ppermute | solution.py:482
  20.4 8.7 %collective-permute-start.5 = (bf16[2,96,256]{2,1,0:T(8,128)(2,1)S(1)}, bf16[2,96,256]{2,1,0:T(8,128)(2,1)S(1)}, u32[]{:S(2)}, u32[]{:S(2)}) collective-permute-start(bf16[2,96,256]{2,1,0:T(8,128)(2,1)S(1)} %get-tuple-element.43), channel_id=1, source_target_pairs={{0,26},{1,5},{2,24},{3,7},{4,30},{5,1},{6,28},{7,3},{8,18},{9,13},... | collective-permute-start | bytes 294920 | tf_op jit(solution)/shard_map/ppermute | solution.py:482
  22.1 8.0 %collective-permute-start.6 = (bf16[2,96,256]{2,1,0:T(8,128)(2,1)S(1)}, bf16[2,96,256]{2,1,0:T(8,128)(2,1)S(1)}, u32[]{:S(2)}, u32[]{:S(2)}) collective-permute-start(bf16[2,96,256]{2,1,0:T(8,128)(2,1)S(1)} %get-tuple-element.44), channel_id=1, source_target_pairs={{0,10},{1,15},{2,8},{3,13},{4,14},{5,11},{6,12},{7,9},{8,2},{9,7},... | collective-permute-start | bytes 294920 | tf_op jit(solution)/shard_map/ppermute | solution.py:482
  25.0 3.3 %copy-start.1 = (f32[16]{0:T(128)S(1)}, f32[16]{0:T(128)}, u32[]{:S(2)}) copy-start(f32[16]{0:T(128)} %roughness.3) | copy-start | bytes 196
  25.0 7.3 %collective-permute-start.7 = (bf16[2,96,256]{2,1,0:T(8,128)(2,1)S(1)}, bf16[2,96,256]{2,1,0:T(8,128)(2,1)S(1)}, u32[]{:S(2)}, u32[]{:S(2)}) collective-permute-start(bf16[2,96,256]{2,1,0:T(8,128)(2,1)S(1)} %get-tuple-element.45), channel_id=1, source_target_pairs={{0,6},{1,9},{2,4},{3,11},{4,2},{5,13},{6,0},{7,15},{8,14},{9,1},{1... | collective-permute-start | bytes 294920 | tf_op jit(solution)/shard_map/ppermute | solution.py:482
  27.1 6.6 %collective-permute-start.8 = (bf16[2,96,256]{2,1,0:T(8,128)(2,1)S(1)}, bf16[2,96,256]{2,1,0:T(8,128)(2,1)S(1)}, u32[]{:S(2)}, u32[]{:S(2)}) collective-permute-start(bf16[2,96,256]{2,1,0:T(8,128)(2,1)S(1)} %get-tuple-element.46), channel_id=1, source_target_pairs={{0,12},{1,31},{2,14},{3,29},{4,8},{5,27},{6,10},{7,25},{8,4},{9,23... | collective-permute-start | bytes 294920 | tf_op jit(solution)/shard_map/ppermute | solution.py:482
  34.2 1.6 %collective-permute-start.11 = (bf16[96,1280]{1,0:T(8,128)(2,1)S(1)}, bf16[96,1280]{1,0:T(8,128)(2,1)S(1)}, u32[]{:S(2)}, u32[]{:S(2)}) collective-permute-start(bf16[96,1280]{1,0:T(8,128)(2,1)S(1)} %get-tuple-element.38), channel_id=1, source_target_pairs={{0,1},{1,0},{2,3},{3,2},{4,5},{5,4},{6,7},{7,6},{8,9},{9,8},{10,11... | collective-permute-start | bytes 737288 | tf_op jit(solution)/shard_map/ppermute | solution.py:498
